TPU v7x, 512 devices: a whole 4x4x16 slice. The times are simulated.
512 devices in a mesh: row: 16 (over y_lo, x, core), col: 32 (over y_hi, z).
Axes of the slice: x: 4, y: 4 (y_hi: 2, y_lo: 2; y = y_hi * 2 + y_lo), z: 16, core: 2. Of those that a mesh axis runs over, the one named last changes fastest.
Arguments:
- amplitudes: float32 [8192, 256], P('row', 'col'), may hold values from -6 to 6
- integrals: float32 [256, 8192], P('row', 'col'), may hold values from -0.375 to 0.375
- occ_counts: int32 [8], replicated, may hold values from 1 to 10, 40 in all
- vir_counts: int32 [8], replicated, may hold values from 1 to 80, 400 in all
Outputs:
- symmetrized: float32 [8192, 8192], P('row', 'col')
Inputs may be any that keep to these rules, and one draw needn't show every extreme that they name: `occ_counts`: counts of occupied orbitals in the 8 irreducible representations, summing to 40. `vir_counts`: counts of virtual orbitals in the 8 irreducible representations, summing to 400.
All inputs are finite; a program needn't handle non-finite values.
Results may differ from a plain program's by a relative error of at most 0.00007.
Values sent between devices are 32-bit elements; how exact they have to be, the bound alone decides.
A program may use at most 64 MiB of HBM per device.

v0:
```python
import jax
import jax.numpy as jnp
from jax import lax
from jax.sharding import PartitionSpec as P

NVIR = 400


def orbital_irreps(orbitals, counts):
    bounds = jnp.cumsum(counts)[:-1]
    return jnp.sum((orbitals[:, None] >= bounds[None, :]).astype(jnp.int32), axis=1)


def pair_labels(positions, occ_counts, vir_counts):
    occ_part = orbital_irreps(positions // NVIR, occ_counts)
    vir_part = orbital_irreps(positions % NVIR, vir_counts)
    return jnp.bitwise_xor(occ_part, vir_part)


def exact_dot(left, right):
    return jnp.dot(left, right, precision=lax.Precision.HIGHEST, preferred_element_type=jnp.float32)


def assemble(received, row_count, narrow):
    grouped = received.reshape(row_count, 2, -1).transpose(1, 0, 2).reshape(2, narrow, narrow)
    return grouped.transpose(1, 0, 2).reshape(narrow, 2 * narrow).T


def per_device(amplitudes, integrals, occ_counts, vir_counts):
    row_count = lax.axis_size("row")
    col_count = lax.axis_size("col")
    row_index = lax.axis_index("row")
    col_index = lax.axis_index("col")
    tall = amplitudes.shape[0]
    narrow = integrals.shape[1]
    row_labels = pair_labels(
        row_index * tall + jnp.arange(tall, dtype=jnp.int32), occ_counts, vir_counts
    )
    col_labels = pair_labels(
        col_index * narrow + jnp.arange(narrow, dtype=jnp.int32), occ_counts, vir_counts
    )
    allowed = row_labels[:, None] == col_labels[None, :]
    parity = col_index % 2
    int_cols = lax.all_gather(integrals, "row", axis=0, tiled=True)
    product = exact_dot(lax.all_gather(amplitudes, "col", axis=1, tiled=True), int_cols)
    flattened = product.reshape(2, row_count, -1)
    oriented = jnp.where(parity == 0, flattened, flattened[::-1])
    outgoing = oriented.transpose(1, 0, 2).reshape(col_count, -1)
    section_one = lax.all_to_all(outgoing, "col", split_axis=0, concat_axis=0, tiled=True)
    section_two = lax.all_to_all(section_one, "row", split_axis=0, concat_axis=0, tiled=True)
    paired = section_two.reshape(row_count, 2, -1)
    paired = jnp.where(parity == 0, paired, paired[:, ::-1]).reshape(col_count, -1)
    section_three = lax.all_to_all(paired, "col", split_axis=0, concat_axis=0, tiled=True)
    arrived = section_three.reshape(row_count, 2, -1)
    arrived = jnp.where(parity == 0, arrived, arrived[:, ::-1]).reshape(col_count, -1)
    mirrored = assemble(arrived, row_count, narrow)
    return jnp.where(allowed, product + mirrored, 0.0)


def solution(mesh):
    placed = (P("row", "col"), P("row", "col"), P(), P())
    return jax.shard_map(
        per_device, mesh=mesh, in_specs=placed, out_specs=P("row", "col"), check_vma=False
    )
```

profile of v0, /device:TPU:32, one launch (start us, length us, event | category | flops | bytes accessed | tf_op | source)
XLA Modules:
  0.0 209.4 jit_solution(9081670944879843364)
XLA Ops:
  0.0 0.7 copy-done
  0.7 81.1 %all_gather.6 = f32[512,256]{0,1:T(8,128)S(1)} all-gather(f32[512,8]{0,1:T(8,128)S(1)} %copy-done), channel_id=1, replica_groups=mesh['row'=16,'col'=32] {'col'}, dimensions={1}, use_global_device_ids=true | all-gather | bytes 540672 | tf_op jit(solution)/shard_map/all_gather | solution.py:45
  81.8 19.5 %all_gather.7 = f32[256,256]{1,0:T(8,128)S(1)} all-gather(f32[16,256]{1,0:T(8,128)S(1)} %copy-done.1), channel_id=1, replica_groups=mesh['row'=16,'col'=32] {'row'}, dimensions={0}, use_global_device_ids=true | all-gather | bytes 278528 | tf_op jit(solution)/shard_map/all_gather | solution.py:44
  101.3 1.0 fusion.8
  102.3 0.1 reshape.88
  102.4 0.4 copy.20
  102.8 1.9 rev.9
  104.7 0.5 select_bitcast_fusion.1
  105.3 0.8 all_to_all.24
  106.1 41.9 %all_to_all.29 = f32[32,1,4096]{2,1,0:T(1,128)S(1)} all-to-all(f32[32,1,4096]{2,1,0:T(1,128)S(1)} %all_to_all.24), channel_id=1, replica_groups=mesh['row'=16,'col'=32] {'col'}, dimensions={0} | all-to-all | bytes 1048576 | tf_op jit(solution)/shard_map/all_to_all | solution.py:49
  147.9 1.2 reduce
  149.2 0.3 all_to_all.20
  149.5 13.5 %all_to_all.30 = f32[16,2,4096]{2,1,0:T(2,128)S(1)} all-to-all(f32[16,2,4096]{2,1,0:T(2,128)S(1)} %all_to_all.20), channel_id=1, replica_groups=mesh['row'=16,'col'=32] {'row'}, dimensions={0} | all-to-all | bytes 1048576 | tf_op jit(solution)/shard_map/all_to_all | solution.py:50
  163.0 1.9 rev.10
  164.9 1.6 all_to_all.25
  166.5 4.5 %all-to-all-start.2 = ((f32[32,1,4096]{2,1,0:T(1,128)}), f32[32,1,4096]{2,1,0:T(1,128)S(1)}, u32[]{:S(2)}, u32[]{:S(2)}) async-start(f32[32,1,4096]{2,1,0:T(1,128)} %all_to_all.25), calls=%async_computation.2 | async-start | bytes 1048576 | tf_op jit(solution)/shard_map/all_to_all | solution.py:53
  171.1 0.6 copy-done.2
  171.8 0.2 reduce-window.9
  171.9 0.7 copy-done.3
  172.6 0.2 reduce-window.6
  172.8 0.1 convert_reduce_fusion.2
  172.9 0.1 convert_reduce_fusion.3
  173.0 0.1 convert_reduce_fusion
  173.1 0.1 convert_reduce_fusion.1
  173.2 30.9 %all-to-all-done.2 = f32[32,1,4096]{2,1,0:T(1,128)S(1)} async-done(((f32[32,1,4096]{2,1,0:T(1,128)}), f32[32,1,4096]{2,1,0:T(1,128)S(1)}, u32[]{:S(2)}, u32[]{:S(2)}) %all-to-all-start.2) | async-done | bytes 524320 | tf_op jit(solution)/shard_map/all_to_all | solution.py:53
  204.1 1.2 reduce.1
  205.3 0.3 reshape.89
  205.6 1.9 rev.11
  207.5 0.3 select_bitcast_fusion
  207.8 0.3 copy.23
  208.3 0.2 copy.24
  208.5 0.9 fusion
  (13 shorter events, 0.2 us)
Async XLA Ops:
  0.0 0.7 copy-start
  0.7 81.1 %copy-start.1 = (f32[16,256]{1,0:T(8,128)S(1)}, f32[16,256]{1,0:T(8,128)}, u32[]{:S(2)}) copy-start(f32[16,256]{1,0:T(8,128)} %param.5) | copy-start | bytes 49156
  166.5 37.5 %all-to-all-start.2 = ((f32[32,1,4096]{2,1,0:T(1,128)}), f32[32,1,4096]{2,1,0:T(1,128)S(1)}, u32[]{:S(2)}, u32[]{:S(2)}) async-start(f32[32,1,4096]{2,1,0:T(1,128)} %all_to_all.25), calls=%async_computation.2 | async-start | bytes 1048576 | tf_op jit(solution)/shard_map/all_to_all | solution.py:53
  171.1 0.7 copy-start.2
  171.9 0.7 copy-start.3
where the time goes:
time: 210 us; the launch traced here: 209 us
  blocking collectives  156 us (74%)
  waiting for transfers between devices  30.9 us (15%)
  local copies, waits for them, and re-layouts  11.9 us (6%)
  other arithmetic  5.09 us (2%)
  starting transfers between devices  4.54 us (2%)
    all_gather x1, blocking collectives, per_device(): lax.all_gather(amplitudes, 'col', axis=1, tiled=True)  81.1 us
    all_to_all x1, blocking collectives, per_device(): lax.all_to_all(outgoing, 'col', split_axis=0, concat_axis=0, tiled=True)  41.9 us
    all_to_all x1, waiting for transfers between devices, per_device(): lax.all_to_all(paired, 'col', split_axis=0, concat_axis=0, tiled=True)  30.9 us
    all_gather x1, blocking collectives, per_device(): int_cols = lax.all_gather(integrals, 'row', axis=0, tiled=True)  19.5 us
    all_to_all x1, blocking collectives, per_device(): lax.all_to_all(section_one, 'row', split_axis=0, concat_axis=0, tiled=True)  13.5 us
    all_to_all x1, starting transfers between devices, per_device(): lax.all_to_all(paired, 'col', split_axis=0, concat_axis=0, tiled=True)  4.54 us
  transfers between devices with their start and end apart: 1, of which 1 were waited for; matrix products, arithmetic and copies ran while one was open for 0% of the time, Pallas kernels for 0%

commit v1 on v0

v1 whole, which is shorter than its diff:
```python
import jax
import jax.numpy as jnp
from jax import lax
from jax.experimental import pallas as pl
from jax.experimental.pallas import tpu as pltpu
from jax.sharding import PartitionSpec as P

NVIR = 400
MESH = pl.DeviceIdType.MESH
F32 = jnp.float32
BF16 = jnp.bfloat16

TREE = (
    (0x000f1e20, 0x00000fe2, 0x00000001, 0x0000000f, 0x00000003, 0x0000012e, 0x00000fe4, 0x0000000d,
     0x00000005, 0x0000012c, 0x000000f6, 0x0000000b, 0x0000012a, 0x00000007, 0x00000009, 0x00000008),
    (0x11102f31, 0x11111112, 0x111110f3, 0x11111110, 0x1111123f, 0x11111114, 0x111110f5, 0x1111111e,
     0x1111123d, 0x11111116, 0x11111107, 0x1111111c, 0x1111123b, 0x11111118, 0x1111111a, 0x11111119),
    (0x22213042, 0x22222223, 0x22222104, 0x22222221, 0x22222340, 0x22222225, 0x22222106, 0x2222222f,
     0x2222234e, 0x22222227, 0x22222218, 0x2222222d, 0x2222234c, 0x22222229, 0x2222222b, 0x2222222a),
    (0x33324153, 0x33333332, 0x33333334, 0x33333215, 0x33333451, 0x33333336, 0x33333330, 0x33333217,
     0x3333345f, 0x3333333e, 0x33333338, 0x3333345d, 0x33333329, 0x3333333a, 0x3333333c, 0x3333333b),
    (0x44435264, 0x44444562, 0x44444443, 0x44444445, 0x44444326, 0x44444441, 0x44444560, 0x44444447,
     0x44444328, 0x4444444f, 0x4444456e, 0x44444449, 0x4444443a, 0x4444444d, 0x4444444c, 0x4444444b),
    (0x55546375, 0x55555554, 0x55555673, 0x55555552, 0x55555556, 0x55555437, 0x55555671, 0x55555558,
     0x55555439, 0x55555550, 0x5555567f, 0x5555555a, 0x5555554b, 0x5555555c, 0x5555555e, 0x5555555d),
    (0x66657486, 0x66666784, 0x66666665, 0x66666782, 0x66666667, 0x66666548, 0x66666663, 0x66666669,
     0x6666654a, 0x66666661, 0x66666780, 0x6666665c, 0x6666666b, 0x6666666d, 0x6666666f, 0x6666666e),
    (0x77768597, 0x77777895, 0x77777776, 0x77777778, 0x77777774, 0x77777659, 0x77777893, 0x77777772,
     0x7777777a, 0x77777891, 0x7777765b, 0x7777777c, 0x7777776d, 0x77777770, 0x7777777f, 0x7777777e),
    (0x888796a8, 0x88888887, 0x888889a6, 0x88888889, 0x888889a4, 0x8888876a, 0x88888885, 0x888889a2,
     0x8888876c, 0x8888888b, 0x88888883, 0x8888888d, 0x8888887e, 0x88888881, 0x88888880, 0x8888888f),
    (0x9998a7b9, 0x99999ab7, 0x9999999a, 0x99999998, 0x9999987b, 0x99999ab5, 0x9999999c, 0x99999996,
     0x9999987d, 0x99999994, 0x99999ab3, 0x99999992, 0x9999999e, 0x99999991, 0x9999998f, 0x99999990),
    (0xaaa9b8ca, 0xaaaaa98c, 0xaaaaaaa9, 0xaaaaabc8, 0xaaaaaaab, 0xaaaaaaa7, 0xaaaaabc6, 0xaaaaaaad,
     0xaaaaa98e, 0xaaaaabc4, 0xaaaaaaa5, 0xaaaaaaa2, 0xaaaaaaaf, 0xaaaaaa90, 0xaaaaaaa3, 0xaaaaaaa1),
    (0xbbbac9db, 0xbbbbbbbc, 0xbbbbbbba, 0xbbbbba9d, 0xbbbbbcd9, 0xbbbbbcd7, 0xbbbbbbbe, 0xbbbbbbb8,
     0xbbbbba9f, 0xbbbbbbb2, 0xbbbbbcd5, 0xbbbbbbb6, 0xbbbbbbb0, 0xbbbbbba1, 0xbbbbbbb4, 0xbbbbbbb3),
    (0xcccbdaec, 0xcccccccd, 0xcccccccb, 0xcccccbae, 0xcccccdea, 0xccccccb2, 0xcccccccf, 0xccccccc9,
     0xcccccba0, 0xcccccde8, 0xccccccc7, 0xcccccde6, 0xccccccc1, 0xccccccc4, 0xccccccc3, 0xccccccc5),
    (0xdddcebfd, 0xdddddddc, 0xddddddde, 0xdddddefb, 0xdddddcbf, 0xddddddd2, 0xddddddd0, 0xddddddda,
     0xdddddcb1, 0xdddddef9, 0xddddddc3, 0xdddddef7, 0xddddddd4, 0xddddddd8, 0xddddddd5, 0xddddddd6),
    (0xeeedfc0e, 0xeeeeedc2, 0xeeeeeeed, 0xeeeeeeef, 0xeeeeef0c, 0xeeeeedc0, 0xeeeeeeeb, 0xeeeeeee1,
     0xeeeeef0a, 0xeeeeeed4, 0xeeeeeee3, 0xeeeeeee5, 0xeeeeeee9, 0xeeeeef08, 0xeeeeeee7, 0xeeeeeee6),
    (0xfffe0d1f, 0xfffffff2, 0xfffffffe, 0xfffffff0, 0xfffff01d, 0xfffffed1, 0xfffffed3, 0xfffffffc,
     0xfffffff4, 0xfffff01b, 0xffffffe5, 0xfffffffa, 0xfffffff6, 0xfffff019, 0xfffffff7, 0xfffffff8),
)

def signed(word):
    return word - (1 << 32) if word >= 1 << 31 else word


def by_z(z, values):
    picked = jnp.int32(signed(values[0]))
    for k in range(1, 16):
        if values[k] != values[0]:
            picked = jnp.where(z == k, jnp.int32(signed(values[k])), picked)
    return picked


def nibble(word, k):
    return (word >> (4 * k)) & 15


def targets(z):
    found = []
    for word in TREE[z]:
        for k in range(1, 8):
            d = (word >> (4 * k)) & 15
            if d != z and d not in found:
                found.append(d)
    return found


SENDS = [sum((word >> (4 * k)) & 15 != z for word in TREE[z] for k in range(1, 8)) for z in range(16)]
MOST = max(SENDS)
TARGETS = [len(targets(z)) for z in range(16)]
SOURCES = [sum(1 << z for z in range(16) if d in targets(z)) for d in range(16)]


def labels(position, base, occ, vir):
    first = base // NVIR
    orbital = jnp.full_like(position, first)
    for k in (1, 2):
        orbital += (position >= (first + k) * NVIR).astype(jnp.int32)
    virtual = position - orbital * NVIR
    occ_part = jnp.zeros_like(position)
    vir_part = jnp.zeros_like(position)
    occ_bound = jnp.int32(0)
    vir_bound = jnp.int32(0)
    for k in range(7):
        occ_bound += occ[k]
        vir_bound += vir[k]
        occ_part += (orbital >= occ_bound).astype(jnp.int32)
        vir_part += (virtual >= vir_bound).astype(jnp.int32)
    return occ_part ^ vir_part


def split(x):
    high = x.astype(BF16)
    return high, (x - high.astype(F32)).astype(BF16)


def product(left, right):
    dims = (((0,), (0,)), ((), ()))
    lh, ll = split(left)
    rh, rl = split(right)
    dot = lambda a, b: lax.dot_general(a, b, dims, preferred_element_type=F32)
    return dot(lh, rh) + (dot(lh, rl) + dot(ll, rh))


def kernel(
    a_hbm, b_hbm, occ, vir, o_ref,
    at, bz, br, bc, ac, row_lab,
    local, at_in, bz_in, br_in, bc_in, ac_in, tree_out, cross_out, br_out, bc_out, ac_out,
):
    row = lax.axis_index("row")
    col = lax.axis_index("col")
    z = col % 16
    yhi = col // 16
    ylo = row // 8

    own = [
        pltpu.make_async_copy(a_hbm.at[:, pl.ds(0, 256)], at.at[col, 0], local.at[0]),
        pltpu.make_async_copy(a_hbm.at[:, pl.ds(256, 256)], at.at[col, 1], local.at[1]),
        pltpu.make_async_copy(b_hbm, bz.at[z], local.at[2]),
        pltpu.make_async_copy(b_hbm, bc.at[row], local.at[3]),
    ]
    for copy in own:
        copy.start()

    barrier = pltpu.get_barrier_semaphore()
    sources = by_z(z, SOURCES)

    def greet_z(d, carry):
        @pl.when(((sources >> d) & 1) == 1)
        def _():
            pl.semaphore_signal(
                barrier, inc=1, device_id={"row": row, "col": yhi * 16 + d}, device_id_type=MESH
            )
        return carry

    def greet_plane(t, carry):
        r, y = t % 16, t // 16

        @pl.when(jnp.logical_or(r != row, y != yhi))
        def _():
            pl.semaphore_signal(
                barrier, inc=1, device_id={"row": r, "col": y * 16 + z}, device_id_type=MESH
            )
        return carry

    lax.fori_loop(0, 16, greet_z, 0)
    lax.fori_loop(0, 32, greet_plane, 0)

    row_pos = row * 512 + lax.broadcasted_iota(jnp.int32, (512, 128), 0)
    row_lab[...] = labels(row_pos, row * 512, occ, vir)

    pl.semaphore_wait(barrier, 31 + by_z(z, TARGETS))
    for copy in own:
        copy.wait()

    def send_tree(s, d, j):
        c = yhi * 16 + s
        dev = {"row": row, "col": yhi * 16 + d}
        pltpu.make_async_remote_copy(
            src_ref=at.at[c], dst_ref=at.at[c], send_sem=tree_out.at[j], recv_sem=at_in.at[c],
            device_id=dev, device_id_type=MESH,
        ).start()
        pltpu.make_async_remote_copy(
            src_ref=bz.at[s], dst_ref=bz.at[s], send_sem=tree_out.at[MOST + j], recv_sem=bz_in.at[s],
            device_id=dev, device_id_type=MESH,
        ).start()

    def cross(s):
        c = yhi * 16 + s
        return pltpu.make_async_remote_copy(
            src_ref=at.at[c], dst_ref=at.at[c], send_sem=cross_out.at[s], recv_sem=at_in.at[c],
            device_id={"row": row, "col": (1 - yhi) * 16 + z}, device_id_type=MESH,
        )

    def to_rows(s, y):
        return pltpu.make_async_remote_copy(
            src_ref=bz.at[s], dst_ref=br.at[row, s % 2], send_sem=br_out.at[2 * s + y],
            recv_sem=br_in.at[2 * row + s % 2],
            device_id={"row": yhi * 8 + s // 2, "col": y * 16 + z}, device_id_type=MESH,
        )

    def mine(s, y):
        return jnp.logical_and(yhi * 8 + s // 2 == row, y == yhi)

    owner = row % 8 == z // 2
    half = z % 2

    def to_plane(s, r):
        c = yhi * 16 + s
        return pltpu.make_async_remote_copy(
            src_ref=at.at[c, half], dst_ref=ac.at[c], send_sem=ac_out.at[16 * s + r], recv_sem=ac_in.at[c],
            device_id={"row": r, "col": ylo * 16 + z}, device_id_type=MESH,
        )

    def own_plane(r):
        return jnp.logical_and(r == row, ylo == yhi)

    def spread(s):
        cross(s).start()
        for y in (0, 1):
            me = mine(s, y)

            @pl.when(me)
            def _():
                pltpu.make_async_copy(bz.at[s], br.at[row, s % 2], br_in.at[2 * row + s % 2]).start()

            @pl.when(jnp.logical_not(me))
            def _():
                to_rows(s, y).start()

        @pl.when(owner)
        def _():
            def one(r, carry):
                me = own_plane(r)

                @pl.when(me)
                def _():
                    c = yhi * 16 + s
                    pltpu.make_async_copy(at.at[c, half], ac.at[c], ac_in.at[c]).start()

                @pl.when(jnp.logical_not(me))
                def _():
                    to_plane(s, r).start()
                return carry

            lax.fori_loop(0, 16, one, 0)

    def to_col(r):
        return pltpu.make_async_remote_copy(
            src_ref=bz.at[z], dst_ref=bc.at[row], send_sem=bc_out.at[r], recv_sem=bc_in.at[row],
            device_id={"row": r, "col": col}, device_id_type=MESH,
        )

    sent = jnp.int32(0)
    for k in range(16):
        word = by_z(z, [TREE[v][k] for v in range(16)])
        s = nibble(word, 0)
        c = yhi * 16 + s
        if k:
            pltpu.make_async_copy(at.at[c], at.at[c], at_in.at[c]).wait()
            pltpu.make_async_copy(bz.at[s], bz.at[s], bz_in.at[s]).wait()

        def forward(i, j):
            d = (word >> (4 * i)) & 15
            there = d != z

            @pl.when(there)
            def _():
                send_tree(s, d, j)
            return j + there.astype(jnp.int32)

        sent = lax.fori_loop(1, 8, forward, sent)
        spread(s)
        if k == 0:
            def give(r, carry):
                @pl.when(r != row)
                def _():
                    to_col(r).start()
                return carry

            lax.fori_loop(0, 16, give, 0)

    def rest(t, carry):
        @pl.when(t != row)
        def _():
            pltpu.make_async_copy(bc.at[t], bc.at[t], bc_in.at[t]).wait()
        c = (1 - yhi) * 16 + t
        pltpu.make_async_copy(at.at[c], at.at[c], at_in.at[c]).wait()
        for e in (0, 1):
            pltpu.make_async_copy(br.at[t, e], br.at[t, e], br_in.at[2 * t + e]).wait()
            pltpu.make_async_copy(ac.at[2 * t + e], ac.at[2 * t + e], ac_in.at[2 * t + e]).wait()
        return carry

    lax.fori_loop(0, 16, rest, 0)

    col_lab = labels(
        col * 256 + lax.broadcasted_iota(jnp.int32, (8, 256), 1), col * 256, occ, vir
    )[:1]
    b_here = bc[...].reshape(256, 256)
    a_here = ac[...].reshape(256, 256)
    for m in (0, 1):
        rows = slice(256 * m, 256 * (m + 1))
        total = product(at[:, m].reshape(256, 256), b_here) + product(br[:, m].reshape(256, 256), a_here)
        lab = row_lab[rows]
        for h in (0, 1):
            lanes = slice(128 * h, 128 * (h + 1))
            o_ref[rows, lanes] = jnp.where(lab == col_lab[:, lanes], total[:, lanes], 0.0)

    def sent_tree(j, carry):
        pltpu.make_async_copy(at.at[0], at.at[0], tree_out.at[j]).wait()
        pltpu.make_async_copy(bz.at[0], bz.at[0], tree_out.at[MOST + j]).wait()
        return carry

    lax.fori_loop(0, by_z(z, SENDS), sent_tree, 0)

    def sent_plane(s, carry):
        cross(s).wait_send()
        for y in (0, 1):
            @pl.when(jnp.logical_not(mine(s, y)))
            def _():
                to_rows(s, y).wait_send()

        @pl.when(s != row)
        def _():
            to_col(s).wait_send()

        @pl.when(owner)
        def _():
            def one(r, carry):
                @pl.when(jnp.logical_not(own_plane(r)))
                def _():
                    to_plane(s, r).wait_send()
                return carry

            lax.fori_loop(0, 16, one, 0)
        return carry

    lax.fori_loop(0, 16, sent_plane, 0)


def per_device(amplitudes, integrals, occ_counts, vir_counts):
    any_space = pl.BlockSpec(memory_space=pl.ANY)
    scalars = pl.BlockSpec(memory_space=pltpu.SMEM)
    dma = pltpu.SemaphoreType.DMA
    return pl.pallas_call(
        kernel,
        out_shape=jax.ShapeDtypeStruct((512, 256), F32),
        in_specs=[any_space, any_space, scalars, scalars],
        out_specs=pl.BlockSpec(memory_space=pltpu.VMEM),
        scratch_shapes=[
            pltpu.VMEM((32, 2, 8, 256), F32),
            pltpu.VMEM((16, 16, 256), F32),
            pltpu.VMEM((16, 2, 16, 256), F32),
            pltpu.VMEM((16, 16, 256), F32),
            pltpu.VMEM((32, 8, 256), F32),
            pltpu.VMEM((512, 128), jnp.int32),
            dma((4,)), dma((32,)), dma((16,)), dma((32,)), dma((16,)), dma((32,)),
            dma((2 * MOST,)), dma((16,)), dma((32,)), dma((16,)), dma((256,)),
        ],
        compiler_params=pltpu.CompilerParams(
            collective_id=0, has_side_effects=True, vmem_limit_bytes=32 * 2**20
        ),
    )(amplitudes.T, integrals, occ_counts, vir_counts)


def solution(mesh):
    placed = (P("row", "col"), P("row", "col"), P(), P())
    return jax.shard_map(
        per_device, mesh=mesh, in_specs=placed, out_specs=P("row", "col"), check_vma=False
    )
```

time: 210 us -> 49.2 us (0.23)
  the two profiles are of different devices: /device:TPU:32 before, /device:TPU:12 now
where the time goes in v1:
time: 49.2 us; the launch traced here: 48.9 us
  Pallas kernels  46 us (93%)
  local copies, waits for them, and re-layouts  2.9 us (6%)
    pallas_call x1, Pallas kernels, per_device(): pl.pallas_call(kernel, out_shape=jax.ShapeDtypeStruct((512, 256), F32), i...  46 us
    unnamed x9, local copies, waits for them, and re-layouts  2.9 us

profile of v1, /device:TPU:12, one launch (start us, length us, event | category | flops | bytes accessed | tf_op | source)
XLA Modules:
  0.0 48.9 jit_solution(9832331588861085150)
XLA Ops:
  0.0 0.0 copy-start.3
  0.0 0.0 copy-start.2
  0.0 0.7 %copy-done.3 = s32[8]{0:T(128)S(1)} copy-done((s32[8]{0:T(128)S(1)}, s32[8]{0:T(128)}, u32[]{:S(2)}) %copy-start.3) | copy-done | bytes 56
  0.7 0.0 copy-done.2
  0.7 0.0 copy-start
  0.7 0.7 %copy-done = f32[512,8]{0,1:T(8,128)S(1)} copy-done((f32[512,8]{0,1:T(8,128)S(1)}, f32[512,8]{0,1:T(8,128)}, u32[]{:S(2)}) %copy-start) | copy-done | bytes 16408
  1.4 0.0 copy-start.1
  1.4 0.7 %copy-done.1 = f32[16,256]{1,0:T(8,128)S(1)} copy-done((f32[16,256]{1,0:T(8,128)S(1)}, f32[16,256]{1,0:T(8,128)}, u32[]{:S(2)}) %copy-start.1) | copy-done | bytes 16408
  2.1 46.0 %shard_map.46 = f32[512,256]{1,0:T(8,128)S(1)} custom-call(f32[8,512]{1,0:T(8,128)S(1)} %bitcast.1, f32[16,256]{1,0:T(8,128)S(1)} %copy-done.1, s32[8]{0:T(128)S(1)} %copy-done.2, s32[8]{0:T(128)S(1)} %copy-done.3), custom_call_target="tpu_custom_call" | custom-call | tf_op jit(solution)/shard_map/pallas_call | solution.py:331
  48.1 0.8 %copy.6 = f32[512,256]{1,0:T(8,128)} copy(f32[512,256]{1,0:T(8,128)S(1)} %shard_map.46) | data formatting | bytes 1048576
Async XLA Ops:
  0.0 0.7 %copy-start.3 = (s32[8]{0:T(128)S(1)}, s32[8]{0:T(128)}, u32[]{:S(2)}) copy-start(s32[8]{0:T(128)} %vir.1) | copy-start | bytes 100
  0.0 0.7 %copy-start.2 = (s32[8]{0:T(128)S(1)}, s32[8]{0:T(128)}, u32[]{:S(2)}) copy-start(s32[8]{0:T(128)} %occ.1) | copy-start | bytes 100
  0.7 0.7 %copy-start = (f32[512,8]{0,1:T(8,128)S(1)}, f32[512,8]{0,1:T(8,128)}, u32[]{:S(2)}) copy-start(f32[512,8]{0,1:T(8,128)} %param.4) | copy-start | bytes 49156
  1.4 0.7 %copy-start.1 = (f32[16,256]{1,0:T(8,128)S(1)}, f32[16,256]{1,0:T(8,128)}, u32[]{:S(2)}) copy-start(f32[16,256]{1,0:T(8,128)} %b_hbm.1) | copy-start | bytes 49156

commit v2 on v1

--- a/solution.py
+++ b/solution.py
@@ -61,6 +61,11 @@
     return (word >> (4 * k)) & 15
 
 
+def quarter(word):
+    first = word & 12
+    return range(first, first + 4)
+
+
 def targets(z):
     found = []
     for word in TREE[z]:
@@ -74,6 +79,11 @@
 SENDS = [sum((word >> (4 * k)) & 15 != z for word in TREE[z] for k in range(1, 8)) for z in range(16)]
 MOST = max(SENDS)
 TARGETS = [len(targets(z)) for z in range(16)]
+LAST = [
+    sum(1 << k for k in range(16) if all(TREE[z][i] & 15 != q for i in range(k + 1, 16) for q in quarter(TREE[z][k])))
+    for z in range(16)
+]
+GROUPS = (0, 1, 3, 2)
 SOURCES = [sum(1 << z for z in range(16) if d in targets(z)) for d in range(16)]
 
 
@@ -109,23 +119,32 @@
 
 
 def kernel(
-    a_hbm, b_hbm, occ, vir, o_ref,
-    at, bz, br, bc, ac, row_lab,
-    local, at_in, bz_in, br_in, bc_in, ac_in, tree_out, cross_out, br_out, bc_out, ac_out,
+    a_hbm, b_hbm, occ_hbm, vir_hbm, o_ref,
+    w, br, bc, ac, row_lab, occ, vir,
+    local, w_in, br_in, bc_in, ac_in, cross_in,
+    tree_out, cross_out, br_out, bc_out, ac_out, pair_out,
 ):
     row = lax.axis_index("row")
     col = lax.axis_index("col")
     z = col % 16
     yhi = col // 16
     ylo = row // 8
+    core = row % 2
 
     own = [
-        pltpu.make_async_copy(a_hbm.at[:, pl.ds(0, 256)], at.at[col, 0], local.at[0]),
-        pltpu.make_async_copy(a_hbm.at[:, pl.ds(256, 256)], at.at[col, 1], local.at[1]),
-        pltpu.make_async_copy(b_hbm, bz.at[z], local.at[2]),
-        pltpu.make_async_copy(b_hbm, bc.at[row], local.at[3]),
+        pltpu.make_async_copy(a_hbm.at[:, pl.ds(256 * h, 256)], w.at[col, h], local.at[h])
+        for h in (0, 1)
+    ] + [
+        pltpu.make_async_copy(b_hbm.at[pl.ds(8 * h, 8)], w.at[col, 2 + h], local.at[2 + h])
+        for h in (0, 1)
     ]
-    for copy in own:
+    small = [
+        pltpu.make_async_copy(occ_hbm, occ, local.at[4]),
+        pltpu.make_async_copy(vir_hbm, vir, local.at[5]),
+        pltpu.make_async_copy(b_hbm.at[pl.ds(0, 8)], bc.at[row, 0], local.at[6]),
+        pltpu.make_async_copy(b_hbm.at[pl.ds(8, 8)], bc.at[row, 1], local.at[7]),
+    ]
+    for copy in own + small:
         copy.start()
 
     barrier = pltpu.get_barrier_semaphore()
@@ -149,11 +168,8 @@
             )
         return carry
 
+    lax.fori_loop(0, 32, greet_plane, 0)
     lax.fori_loop(0, 16, greet_z, 0)
-    lax.fori_loop(0, 32, greet_plane, 0)
-
-    row_pos = row * 512 + lax.broadcasted_iota(jnp.int32, (512, 128), 0)
-    row_lab[...] = labels(row_pos, row * 512, occ, vir)
 
     pl.semaphore_wait(barrier, 31 + by_z(z, TARGETS))
     for copy in own:
@@ -161,90 +177,67 @@
 
     def send_tree(s, d, j):
         c = yhi * 16 + s
-        dev = {"row": row, "col": yhi * 16 + d}
         pltpu.make_async_remote_copy(
-            src_ref=at.at[c], dst_ref=at.at[c], send_sem=tree_out.at[j], recv_sem=at_in.at[c],
-            device_id=dev, device_id_type=MESH,
-        ).start()
-        pltpu.make_async_remote_copy(
-            src_ref=bz.at[s], dst_ref=bz.at[s], send_sem=tree_out.at[MOST + j], recv_sem=bz_in.at[s],
-            device_id=dev, device_id_type=MESH,
+            src_ref=w.at[c], dst_ref=w.at[c], send_sem=tree_out.at[j], recv_sem=w_in.at[s],
+            device_id={"row": row, "col": yhi * 16 + d}, device_id_type=MESH,
         ).start()
 
     def cross(s):
         c = yhi * 16 + s
         return pltpu.make_async_remote_copy(
-            src_ref=at.at[c], dst_ref=at.at[c], send_sem=cross_out.at[s], recv_sem=at_in.at[c],
-            device_id={"row": row, "col": (1 - yhi) * 16 + z}, device_id_type=MESH,
+            src_ref=w.at[c, pl.ds(0, 2)], dst_ref=w.at[c, pl.ds(0, 2)], send_sem=cross_out,
+            recv_sem=cross_in, device_id={"row": row, "col": (1 - yhi) * 16 + z}, device_id_type=MESH,
         )
 
     def to_rows(s, y):
-        return pltpu.make_async_remote_copy(
-            src_ref=bz.at[s], dst_ref=br.at[row, s % 2], send_sem=br_out.at[2 * s + y],
-            recv_sem=br_in.at[2 * row + s % 2],
-            device_id={"row": yhi * 8 + s // 2, "col": y * 16 + z}, device_id_type=MESH,
-        )
-
-    def mine(s, y):
-        return jnp.logical_and(yhi * 8 + s // 2 == row, y == yhi)
+        r = yhi * 8 + s // 2
+        source = w.at[yhi * 16 + s, pl.ds(2, 2)]
+        me = jnp.logical_and(r == row, y == yhi)
+
+        @pl.when(me)
+        def _():
+            pltpu.make_async_copy(source, br.at[row, s % 2], br_in).start()
+
+        @pl.when(jnp.logical_not(me))
+        def _():
+            pltpu.make_async_remote_copy(
+                src_ref=source, dst_ref=br.at[row, s % 2], send_sem=br_out, recv_sem=br_in,
+                device_id={"row": r, "col": y * 16 + z}, device_id_type=MESH,
+            ).start()
 
     owner = row % 8 == z // 2
     half = z % 2
 
-    def to_plane(s, r):
-        c = yhi * 16 + s
-        return pltpu.make_async_remote_copy(
-            src_ref=at.at[c, half], dst_ref=ac.at[c], send_sem=ac_out.at[16 * s + r], recv_sem=ac_in.at[c],
-            device_id={"row": r, "col": ylo * 16 + z}, device_id_type=MESH,
-        )
-
-    def own_plane(r):
-        return jnp.logical_and(r == row, ylo == yhi)
-
-    def spread(s):
-        cross(s).start()
-        for y in (0, 1):
-            me = mine(s, y)
+    def to_plane(g):
+        c = yhi * 16 + 4 * g
+        source = w.at[pl.ds(c, 4), half]
+
+        def one(chip, carry):
+            r = 2 * chip + core
+            me = jnp.logical_and(r == row, ylo == yhi)
 
             @pl.when(me)
             def _():
-                pltpu.make_async_copy(bz.at[s], br.at[row, s % 2], br_in.at[2 * row + s % 2]).start()
+                pltpu.make_async_copy(source, ac.at[pl.ds(c, 4)], ac_in.at[yhi * 4 + g]).start()
 
             @pl.when(jnp.logical_not(me))
             def _():
-                to_rows(s, y).start()
-
-        @pl.when(owner)
-        def _():
-            def one(r, carry):
-                me = own_plane(r)
-
-                @pl.when(me)
-                def _():
-                    c = yhi * 16 + s
-                    pltpu.make_async_copy(at.at[c, half], ac.at[c], ac_in.at[c]).start()
-
-                @pl.when(jnp.logical_not(me))
-                def _():
-                    to_plane(s, r).start()
-                return carry
-
-            lax.fori_loop(0, 16, one, 0)
-
-    def to_col(r):
-        return pltpu.make_async_remote_copy(
-            src_ref=bz.at[z], dst_ref=bc.at[row], send_sem=bc_out.at[r], recv_sem=bc_in.at[row],
-            device_id={"row": r, "col": col}, device_id_type=MESH,
-        )
-
+                pltpu.make_async_remote_copy(
+                    src_ref=source, dst_ref=ac.at[pl.ds(c, 4)], send_sem=ac_out.at[g],
+                    recv_sem=ac_in.at[yhi * 4 + g],
+                    device_id={"row": r, "col": ylo * 16 + z}, device_id_type=MESH,
+                ).start()
+            return carry
+
+        lax.fori_loop(0, 8, one, 0)
+
+    last = by_z(z, LAST)
     sent = jnp.int32(0)
     for k in range(16):
         word = by_z(z, [TREE[v][k] for v in range(16)])
         s = nibble(word, 0)
-        c = yhi * 16 + s
         if k:
-            pltpu.make_async_copy(at.at[c], at.at[c], at_in.at[c]).wait()
-            pltpu.make_async_copy(bz.at[s], bz.at[s], bz_in.at[s]).wait()
+            pltpu.make_async_copy(w.at[s], w.at[s], w_in.at[s]).wait()
 
         def forward(i, j):
             d = (word >> (4 * i)) & 15
@@ -256,28 +249,55 @@
             return j + there.astype(jnp.int32)
 
         sent = lax.fori_loop(1, 8, forward, sent)
-        spread(s)
+        cross(s).start()
+        to_rows(s, 0)
+        to_rows(s, 1)
+
+        @pl.when(jnp.logical_and(owner, ((last >> k) & 1) == 1))
+        def _():
+            to_plane(s // 4)
+
         if k == 0:
             def give(r, carry):
                 @pl.when(r != row)
                 def _():
-                    to_col(r).start()
+                    pltpu.make_async_remote_copy(
+                        src_ref=w.at[col, pl.ds(2, 2)], dst_ref=bc.at[row], send_sem=bc_out,
+                        recv_sem=bc_in, device_id={"row": r, "col": col}, device_id_type=MESH,
+                    ).start()
                 return carry
 
             lax.fori_loop(0, 16, give, 0)
-
-    def rest(t, carry):
-        @pl.when(t != row)
-        def _():
-            pltpu.make_async_copy(bc.at[t], bc.at[t], bc_in.at[t]).wait()
-        c = (1 - yhi) * 16 + t
-        pltpu.make_async_copy(at.at[c], at.at[c], at_in.at[c]).wait()
-        for e in (0, 1):
-            pltpu.make_async_copy(br.at[t, e], br.at[t, e], br_in.at[2 * t + e]).wait()
-            pltpu.make_async_copy(ac.at[2 * t + e], ac.at[2 * t + e], ac_in.at[2 * t + e]).wait()
-        return carry
-
-    lax.fori_loop(0, 16, rest, 0)
+            for copy in small:
+                copy.wait()
+            row_pos = row * 512 + lax.broadcasted_iota(jnp.int32, (512, 128), 0)
+            row_lab[...] = labels(row_pos, row * 512, occ, vir)
+
+    first = core == (z // 2) % 2
+
+    def group(t):
+        return ac.at[pl.ds(4 * t, 4)]
+
+    @pl.when(first)
+    def _():
+        for g in GROUPS:
+            for y in (0, 1):
+                t = 4 * y + g
+                pltpu.make_async_copy(group(t), group(t), ac_in.at[t]).wait()
+                pltpu.make_async_remote_copy(
+                    src_ref=group(t), dst_ref=group(t), send_sem=pair_out.at[t],
+                    recv_sem=ac_in.at[t], device_id={"row": 2 * (row // 2) + 1 - core, "col": col},
+                    device_id_type=MESH,
+                ).start()
+
+    pltpu.make_async_copy(bc.at[pl.ds(0, 15)], bc.at[pl.ds(0, 15)], bc_in).wait()
+    pltpu.make_async_copy(ac, ac, cross_in).wait()
+    pltpu.make_async_copy(br, br, br_in).wait()
+
+    @pl.when(jnp.logical_not(first))
+    def _():
+        for t in range(8):
+            pltpu.make_async_copy(group(t), group(t), ac_in.at[t]).wait()
 
     col_lab = labels(
         col * 256 + lax.broadcasted_iota(jnp.int32, (8, 256), 1), col * 256, occ, vir
@@ -286,67 +306,69 @@
     a_here = ac[...].reshape(256, 256)
     for m in (0, 1):
         rows = slice(256 * m, 256 * (m + 1))
-        total = product(at[:, m].reshape(256, 256), b_here) + product(br[:, m].reshape(256, 256), a_here)
+        total = product(w[:, m].reshape(256, 256), b_here) + product(br[:, m].reshape(256, 256), a_here)
         lab = row_lab[rows]
         for h in (0, 1):
             lanes = slice(128 * h, 128 * (h + 1))
             o_ref[rows, lanes] = jnp.where(lab == col_lab[:, lanes], total[:, lanes], 0.0)
 
     def sent_tree(j, carry):
-        pltpu.make_async_copy(at.at[0], at.at[0], tree_out.at[j]).wait()
-        pltpu.make_async_copy(bz.at[0], bz.at[0], tree_out.at[MOST + j]).wait()
+        pltpu.make_async_copy(w.at[0], w.at[0], tree_out.at[j]).wait()
         return carry
 
     lax.fori_loop(0, by_z(z, SENDS), sent_tree, 0)
-
-    def sent_plane(s, carry):
-        cross(s).wait_send()
-        for y in (0, 1):
-            @pl.when(jnp.logical_not(mine(s, y)))
-            def _():
-                to_rows(s, y).wait_send()
-
-        @pl.when(s != row)
-        def _():
-            to_col(s).wait_send()
-
-        @pl.when(owner)
-        def _():
-            def one(r, carry):
-                @pl.when(jnp.logical_not(own_plane(r)))
-                def _():
-                    to_plane(s, r).wait_send()
-                return carry
-
-            lax.fori_loop(0, 16, one, 0)
-        return carry
-
-    lax.fori_loop(0, 16, sent_plane, 0)
+    pltpu.make_async_copy(ac, ac, cross_out).wait()
+    pltpu.make_async_copy(bc.at[pl.ds(0, 15)], bc.at[pl.ds(0, 15)], bc_out).wait()
+
+    @pl.when(ylo == yhi)
+    def _():
+        pltpu.make_async_copy(br.at[pl.ds(0, 15)], br.at[pl.ds(0, 15)], br_out).wait()
+
+    @pl.when(ylo != yhi)
+    def _():
+        pltpu.make_async_copy(br, br, br_out).wait()
+
+    @pl.when(owner)
+    def _():
+        for g in range(4):
+            @pl.when(ylo == yhi)
+            def _():
+                pltpu.make_async_copy(ac.at[pl.ds(0, 28)], ac.at[pl.ds(0, 28)], ac_out.at[g]).wait()
+
+            @pl.when(ylo != yhi)
+            def _():
+                pltpu.make_async_copy(ac, ac, ac_out.at[g]).wait()
+
+    @pl.when(first)
+    def _():
+        for t in range(8):
+            pltpu.make_async_copy(group(t), group(t), pair_out.at[t]).wait()
 
 
 def per_device(amplitudes, integrals, occ_counts, vir_counts):
-    any_space = pl.BlockSpec(memory_space=pl.ANY)
-    scalars = pl.BlockSpec(memory_space=pltpu.SMEM)
+    arrays = (amplitudes.T, integrals, occ_counts, vir_counts)
+    hbm = pl.BlockSpec(memory_space=pltpu.HBM)
     dma = pltpu.SemaphoreType.DMA
     return pl.pallas_call(
         kernel,
         out_shape=jax.ShapeDtypeStruct((512, 256), F32),
-        in_specs=[any_space, any_space, scalars, scalars],
+        in_specs=[hbm, hbm, hbm, hbm],
         out_specs=pl.BlockSpec(memory_space=pltpu.VMEM),
         scratch_shapes=[
-            pltpu.VMEM((32, 2, 8, 256), F32),
-            pltpu.VMEM((16, 16, 256), F32),
-            pltpu.VMEM((16, 2, 16, 256), F32),
-            pltpu.VMEM((16, 16, 256), F32),
+            pltpu.VMEM((32, 4, 8, 256), F32),
+            pltpu.VMEM((16, 2, 2, 8, 256), F32),
+            pltpu.VMEM((16, 2, 8, 256), F32),
             pltpu.VMEM((32, 8, 256), F32),
             pltpu.VMEM((512, 128), jnp.int32),
-            dma((4,)), dma((32,)), dma((16,)), dma((32,)), dma((16,)), dma((32,)),
-            dma((2 * MOST,)), dma((16,)), dma((32,)), dma((16,)), dma((256,)),
+            pltpu.SMEM((8,), jnp.int32),
+            pltpu.SMEM((8,), jnp.int32),
+            dma((8,)), dma((16,)), dma, dma, dma((8,)), dma,
+            dma((MOST,)), dma, dma, dma, dma((4,)), dma((8,)),
         ],
         compiler_params=pltpu.CompilerParams(
             collective_id=0, has_side_effects=True, vmem_limit_bytes=32 * 2**20
         ),
-    )(amplitudes.T, integrals, occ_counts, vir_counts)
+    )(*[pltpu.with_memory_space_constraint(v, pltpu.HBM) for v in arrays])
 
 
 def solution(mesh):

time: 49.2 us -> 41.9 us (0.85)
  Pallas kernels: 46 us -> 41 us
  local copies, waits for them, and re-layouts: 2.9 us -> 0.8 us
    pallas_call x1, Pallas kernels: 46 us -> 41 us  [per_device(): pl.pallas_call(kernel, out_shape=jax.ShapeDtypeStruct((512, 256), F32), i...]
    unnamed x9 -> x1, local copies, waits for them, and re-layouts: 2.9 us -> 0.8 us
where the time goes in v2:
time: 41.9 us; the launch traced here: 41.8 us
  Pallas kernels  41 us (98%)
  local copies, waits for them, and re-layouts  0.8 us (2%)
    pallas_call x1, Pallas kernels, per_device(): pl.pallas_call(kernel, out_shape=jax.ShapeDtypeStruct((512, 256), F32), i...  41 us

profile of v2, /device:TPU:12, one launch (start us, length us, event | category | flops | bytes accessed | tf_op | source)
XLA Modules:
  0.0 41.8 jit_solution(9991639159158842049)
XLA Ops:
  0.0 41.0 %shard_map.46 = f32[512,256]{1,0:T(8,128)S(1)} custom-call(f32[8,512]{1,0:T(8,128)} %bitcast.1, f32[16,256]{1,0:T(8,128)} %b_hbm.1, s32[8]{0:T(128)} %occ_hbm.1, s32[8]{0:T(128)} %vir_hbm.1), custom_call_target="tpu_custom_call" | custom-call | tf_op jit(solution)/shard_map/pallas_call | solution.py:352
  41.0 0.8 %copy.6 = f32[512,256]{1,0:T(8,128)} copy(f32[512,256]{1,0:T(8,128)S(1)} %shard_map.46) | data formatting | bytes 1048576

commit v3 on v2

--- a/solution.py
+++ b/solution.py
@@ -6,43 +6,44 @@
 from jax.sharding import PartitionSpec as P
 
 NVIR = 400
+SPAN = 2
 MESH = pl.DeviceIdType.MESH
 F32 = jnp.float32
 BF16 = jnp.bfloat16
 
 TREE = (
-    (0x000f1e20, 0x00000fe2, 0x00000001, 0x0000000f, 0x00000003, 0x0000012e, 0x00000fe4, 0x0000000d,
-     0x00000005, 0x0000012c, 0x000000f6, 0x0000000b, 0x0000012a, 0x00000007, 0x00000009, 0x00000008),
-    (0x11102f31, 0x11111112, 0x111110f3, 0x11111110, 0x1111123f, 0x11111114, 0x111110f5, 0x1111111e,
-     0x1111123d, 0x11111116, 0x11111107, 0x1111111c, 0x1111123b, 0x11111118, 0x1111111a, 0x11111119),
-    (0x22213042, 0x22222223, 0x22222104, 0x22222221, 0x22222340, 0x22222225, 0x22222106, 0x2222222f,
-     0x2222234e, 0x22222227, 0x22222218, 0x2222222d, 0x2222234c, 0x22222229, 0x2222222b, 0x2222222a),
-    (0x33324153, 0x33333332, 0x33333334, 0x33333215, 0x33333451, 0x33333336, 0x33333330, 0x33333217,
-     0x3333345f, 0x3333333e, 0x33333338, 0x3333345d, 0x33333329, 0x3333333a, 0x3333333c, 0x3333333b),
-    (0x44435264, 0x44444562, 0x44444443, 0x44444445, 0x44444326, 0x44444441, 0x44444560, 0x44444447,
-     0x44444328, 0x4444444f, 0x4444456e, 0x44444449, 0x4444443a, 0x4444444d, 0x4444444c, 0x4444444b),
-    (0x55546375, 0x55555554, 0x55555673, 0x55555552, 0x55555556, 0x55555437, 0x55555671, 0x55555558,
-     0x55555439, 0x55555550, 0x5555567f, 0x5555555a, 0x5555554b, 0x5555555c, 0x5555555e, 0x5555555d),
-    (0x66657486, 0x66666784, 0x66666665, 0x66666782, 0x66666667, 0x66666548, 0x66666663, 0x66666669,
-     0x6666654a, 0x66666661, 0x66666780, 0x6666665c, 0x6666666b, 0x6666666d, 0x6666666f, 0x6666666e),
-    (0x77768597, 0x77777895, 0x77777776, 0x77777778, 0x77777774, 0x77777659, 0x77777893, 0x77777772,
-     0x7777777a, 0x77777891, 0x7777765b, 0x7777777c, 0x7777776d, 0x77777770, 0x7777777f, 0x7777777e),
-    (0x888796a8, 0x88888887, 0x888889a6, 0x88888889, 0x888889a4, 0x8888876a, 0x88888885, 0x888889a2,
-     0x8888876c, 0x8888888b, 0x88888883, 0x8888888d, 0x8888887e, 0x88888881, 0x88888880, 0x8888888f),
-    (0x9998a7b9, 0x99999ab7, 0x9999999a, 0x99999998, 0x9999987b, 0x99999ab5, 0x9999999c, 0x99999996,
-     0x9999987d, 0x99999994, 0x99999ab3, 0x99999992, 0x9999999e, 0x99999991, 0x9999998f, 0x99999990),
-    (0xaaa9b8ca, 0xaaaaa98c, 0xaaaaaaa9, 0xaaaaabc8, 0xaaaaaaab, 0xaaaaaaa7, 0xaaaaabc6, 0xaaaaaaad,
-     0xaaaaa98e, 0xaaaaabc4, 0xaaaaaaa5, 0xaaaaaaa2, 0xaaaaaaaf, 0xaaaaaa90, 0xaaaaaaa3, 0xaaaaaaa1),
-    (0xbbbac9db, 0xbbbbbbbc, 0xbbbbbbba, 0xbbbbba9d, 0xbbbbbcd9, 0xbbbbbcd7, 0xbbbbbbbe, 0xbbbbbbb8,
-     0xbbbbba9f, 0xbbbbbbb2, 0xbbbbbcd5, 0xbbbbbbb6, 0xbbbbbbb0, 0xbbbbbba1, 0xbbbbbbb4, 0xbbbbbbb3),
-    (0xcccbdaec, 0xcccccccd, 0xcccccccb, 0xcccccbae, 0xcccccdea, 0xccccccb2, 0xcccccccf, 0xccccccc9,
-     0xcccccba0, 0xcccccde8, 0xccccccc7, 0xcccccde6, 0xccccccc1, 0xccccccc4, 0xccccccc3, 0xccccccc5),
-    (0xdddcebfd, 0xdddddddc, 0xddddddde, 0xdddddefb, 0xdddddcbf, 0xddddddd2, 0xddddddd0, 0xddddddda,
-     0xdddddcb1, 0xdddddef9, 0xddddddc3, 0xdddddef7, 0xddddddd4, 0xddddddd8, 0xddddddd5, 0xddddddd6),
-    (0xeeedfc0e, 0xeeeeedc2, 0xeeeeeeed, 0xeeeeeeef, 0xeeeeef0c, 0xeeeeedc0, 0xeeeeeeeb, 0xeeeeeee1,
-     0xeeeeef0a, 0xeeeeeed4, 0xeeeeeee3, 0xeeeeeee5, 0xeeeeeee9, 0xeeeeef08, 0xeeeeeee7, 0xeeeeeee6),
-    (0xfffe0d1f, 0xfffffff2, 0xfffffffe, 0xfffffff0, 0xfffff01d, 0xfffffed1, 0xfffffed3, 0xfffffffc,
-     0xfffffff4, 0xfffff01b, 0xffffffe5, 0xfffffffa, 0xfffffff6, 0xfffff019, 0xfffffff7, 0xfffffff8),
+    (0x0000dc20, 0x000002cf, 0x000000f4, 0x000000d2, 0x0000031d, 0x0000e21b, 0x000000f3, 0x000000f6,
+     0x0000001a, 0x0000000e, 0x00000018, 0x000000d5, 0x00000001, 0x0000000c, 0x00000009, 0x00000007),
+    (0x11124bf1, 0x11111112, 0x1111204e, 0x11111105, 0x111d320c, 0x11111114, 0x11111119, 0x11111110,
+     0x1111112d, 0x11111113, 0x111113db, 0x1111116f, 0x111111d6, 0x1111111a, 0x11111118, 0x111111f7),
+    (0x22213042, 0x22222214, 0x22223510, 0x22222213, 0x22222221, 0x22222136, 0x2222222f, 0x22222235,
+     0x22222228, 0x2222222e, 0x222222f9, 0x222222ec, 0x2222222b, 0x22222227, 0x2222222d, 0x2222222a),
+    (0x33504623, 0x33333334, 0x33333382, 0x3333351f, 0x33321407, 0x33333348, 0x33333330, 0x33333339,
+     0x33333346, 0x33333331, 0x3333334d, 0x333333fa, 0x33333335, 0x3333333c, 0x3333333e, 0x3333333b),
+    (0x44532604, 0x44444425, 0x44444462, 0x44444443, 0x44447531, 0x4444235a, 0x4444653e, 0x44444449,
+     0x44444457, 0x4444444c, 0x44444458, 0x44444440, 0x4444444f, 0x44444446, 0x4444444d, 0x4444444b),
+    (0x55574615, 0x55555574, 0x55555553, 0x55555540, 0x55555559, 0x5555547f, 0x55555561, 0x5555555c,
+     0x5555555a, 0x55555552, 0x55555556, 0x5555555e, 0x5555555b, 0x55555557, 0x5555555d, 0x55555558),
+    (0x66662806, 0x66666895, 0x66666684, 0x66666329, 0x66666973, 0x6666574c, 0x66666572, 0x6666687a,
+     0x6666664b, 0x6666667d, 0x66666661, 0x66666668, 0x6666666e, 0x66666660, 0x66666667, 0x6666666f),
+    (0x7779e3a7, 0x777777a5, 0x7777b459, 0x77777774, 0x77777596, 0x7777775b, 0x7777b8a3, 0x77777768,
+     0x7777777c, 0x777777a2, 0x7777777e, 0x77778a91, 0x7777777f, 0x7777777a, 0x7777777d, 0x77777770),
+    (0x8893b028, 0x8888c7a6, 0x88888889, 0x8888886b, 0x888888b5, 0x888888a4, 0x8888885d, 0x88888867,
+     0x88888892, 0x88888883, 0x8888888c, 0x8888888a, 0x88888880, 0x8888888e, 0x8888888f, 0x88888881),
+    (0x998a7169, 0x9999a78b, 0x9999996a, 0x99999a78, 0x99999987, 0x99999995, 0x999999bd, 0x99999990,
+     0x999999c3, 0x9999999e, 0x99999996, 0x9999999c, 0x99999992, 0x99999991, 0x9999999f, 0x99999994),
+    (0xaaac940a, 0xaaaaac09, 0xaaaaa86d, 0xaaaaaab7, 0xaaaaaacb, 0xaaaaa97e, 0xaaaaaaa8, 0xaaaaaaa6,
+     0xaaaaa98c, 0xaaaaaaf5, 0xaaaaa870, 0xaaaaa98f, 0xaaaaa9b4, 0xaaaaaaa3, 0xaaaaaaa2, 0xaaaaaaa1),
+    (0xbbbbb09b, 0xbbbbbbac, 0xbbbbbed8, 0xbbbbbbce, 0xbbbbbb60, 0xbbbbbdc7, 0xbbbbbbba, 0xbbbbbbb1,
+     0xbbbbbbb9, 0xbbbbbbc5, 0xbbbbbbbf, 0xbbbbbbb2, 0xbbbbbbbd, 0xbbbbbbb6, 0xbbbbbbb3, 0xbbbbbbb4),
+    (0xccccb16c, 0xccccc9ed, 0xccccc9b0, 0xcccccbda, 0xccccccbf, 0xccccccd9, 0xcccccc8e, 0xccccccb6,
+     0xcccccccb, 0xccccccc7, 0xccccccc2, 0xccccccc8, 0xccccccc1, 0xccccccc4, 0xccccccc5, 0xccccccc3),
+    (0xddddca0d, 0xdddddabe, 0xdddddea0, 0xddddddaf, 0xddddddea, 0xdddfecb2, 0xddddddc8, 0xdddddec1,
+     0xddddddc4, 0xdddddde9, 0xddddddfc, 0xdddddde5, 0xddddddd7, 0xdddddddb, 0xddddddd6, 0xddddddd3),
+    (0xeeeed1fe, 0xeeeeeedf, 0xeeeeeefd, 0xeeeeeef0, 0xeeeeeefb, 0xeeeeeee7, 0xeeeeeee4, 0xeeeeeef8,
+     0xeeeeeeea, 0xeeeeeee2, 0xeeeeeed3, 0xeeeeeee1, 0xeeeeeee6, 0xeeeeeee9, 0xeeeeeeec, 0xeeeeeee5),
+    (0xffff3e0f, 0xfffffffe, 0xfffffd01, 0xfffffed4, 0xffffffe3, 0xffffffe6, 0xfffffffd, 0xfffffff0,
+     0xfffffffb, 0xfffffff2, 0xfffffff9, 0xfffffff8, 0xfffffff7, 0xfffffff5, 0xfffffffa, 0xfffffffc),
 )
 
 def signed(word):
@@ -62,8 +63,8 @@
 
 
 def quarter(word):
-    first = word & 12
-    return range(first, first + 4)
+    first = (word & 15) // SPAN * SPAN
+    return range(first, first + SPAN)
 
 
 def targets(z):
@@ -83,7 +84,7 @@
     sum(1 << k for k in range(16) if all(TREE[z][i] & 15 != q for i in range(k + 1, 16) for q in quarter(TREE[z][k])))
     for z in range(16)
 ]
-GROUPS = (0, 1, 3, 2)
+GROUPS = tuple(q // SPAN for q in (0, 2, 4, 6, 14, 12, 10, 8)) if SPAN == 2 else (0, 1, 3, 2)
 SOURCES = [sum(1 << z for z in range(16) if d in targets(z)) for d in range(16)]
 
 
@@ -121,7 +122,7 @@
 def kernel(
     a_hbm, b_hbm, occ_hbm, vir_hbm, o_ref,
     w, br, bc, ac, row_lab, occ, vir,
-    local, w_in, br_in, bc_in, ac_in, cross_in,
+    local, w_in, br_in, bc_in, ac_in, cross_in, ready,
     tree_out, cross_out, br_out, bc_out, ac_out, pair_out,
 ):
     row = lax.axis_index("row")
@@ -130,6 +131,7 @@
     yhi = col // 16
     ylo = row // 8
     core = row % 2
+    x = row // 2 % 4
 
     own = [
         pltpu.make_async_copy(a_hbm.at[:, pl.ds(256 * h, 256)], w.at[col, h], local.at[h])
@@ -158,20 +160,42 @@
             )
         return carry
 
-    def greet_plane(t, carry):
-        r, y = t % 16, t // 16
-
-        @pl.when(jnp.logical_or(r != row, y != yhi))
-        def _():
-            pl.semaphore_signal(
-                barrier, inc=1, device_id={"row": r, "col": y * 16 + z}, device_id_type=MESH
-            )
-        return carry
-
-    lax.fori_loop(0, 32, greet_plane, 0)
+    other = {"row": row + 1 - 2 * core, "col": col}
+    peers = [other]
+    peers += [{"row": ylo * 8 + (x + k) % 4 * 2 + core, "col": col} for k in (1, 2, 3)]
+    peers += [
+        {"row": (ylo + k % 2) % 2 * 8 + x * 2 + core, "col": (yhi + k // 2) % 2 * 16 + z} for k in (1, 2, 3)
+    ]
+    late = z >= 8
+
+    @pl.when(late)
+    def _():
+        for peer in peers:
+            pl.semaphore_signal(barrier, inc=1, device_id=peer, device_id_type=MESH)
+
+    @pl.when(jnp.logical_not(late))
+    def _():
+        def greet_plane(t, carry):
+            r, y = t % 16, t // 16
+
+            @pl.when(jnp.logical_or(r != row, y != yhi))
+            def _():
+                pl.semaphore_signal(
+                    barrier, inc=1, device_id={"row": r, "col": y * 16 + z}, device_id_type=MESH
+                )
+            return carry
+
+        lax.fori_loop(0, 32, greet_plane, 0)
+
     lax.fori_loop(0, 16, greet_z, 0)
 
-    pl.semaphore_wait(barrier, 31 + by_z(z, TARGETS))
+    pl.semaphore_wait(barrier, jnp.where(late, 7, 31) + by_z(z, TARGETS))
+
+    @pl.when(late)
+    def _():
+        for peer in peers:
+            pl.semaphore_signal(ready.at[0], inc=1, device_id=peer, device_id_type=MESH)
+
     for copy in own:
         copy.wait()
 
@@ -209,8 +233,9 @@
     half = z % 2
 
     def to_plane(g):
-        c = yhi * 16 + 4 * g
-        source = w.at[pl.ds(c, 4), half]
+        c = yhi * 16 + SPAN * g
+        t = yhi * (16 // SPAN) + g
+        source = w.at[pl.ds(c, SPAN), half]
 
         def one(chip, carry):
             r = 2 * chip + core
@@ -218,13 +243,13 @@
 
             @pl.when(me)
             def _():
-                pltpu.make_async_copy(source, ac.at[pl.ds(c, 4)], ac_in.at[yhi * 4 + g]).start()
+                pltpu.make_async_copy(source, ac.at[pl.ds(c, SPAN)], ac_in.at[t]).start()
 
             @pl.when(jnp.logical_not(me))
             def _():
                 pltpu.make_async_remote_copy(
-                    src_ref=source, dst_ref=ac.at[pl.ds(c, 4)], send_sem=ac_out.at[g],
-                    recv_sem=ac_in.at[yhi * 4 + g],
+                    src_ref=source, dst_ref=ac.at[pl.ds(c, SPAN)], send_sem=ac_out.at[g],
+                    recv_sem=ac_in.at[t],
                     device_id={"row": r, "col": ylo * 16 + z}, device_id_type=MESH,
                 ).start()
             return carry
@@ -249,13 +274,19 @@
             return j + there.astype(jnp.int32)
 
         sent = lax.fori_loop(1, 8, forward, sent)
+        if k == 0:
+            @pl.when(late)
+            def _():
+                pl.semaphore_wait(ready.at[0], 7)
+                pl.semaphore_signal(ready.at[1], inc=1, device_id=other, device_id_type=MESH)
+                pl.semaphore_wait(ready.at[1], 1)
         cross(s).start()
         to_rows(s, 0)
         to_rows(s, 1)
 
         @pl.when(jnp.logical_and(owner, ((last >> k) & 1) == 1))
         def _():
-            to_plane(s // 4)
+            to_plane(s // SPAN)
 
         if k == 0:
             def give(r, carry):
@@ -276,13 +307,13 @@
     first = core == (z // 2) % 2
 
     def group(t):
-        return ac.at[pl.ds(4 * t, 4)]
+        return ac.at[pl.ds(SPAN * t, SPAN)]
 
     @pl.when(first)
     def _():
         for g in GROUPS:
             for y in (0, 1):
-                t = 4 * y + g
+                t = 16 // SPAN * y + g
                 pltpu.make_async_copy(group(t), group(t), ac_in.at[t]).wait()
                 pltpu.make_async_remote_copy(
                     src_ref=group(t), dst_ref=group(t), send_sem=pair_out.at[t],
@@ -296,7 +327,7 @@
 
     @pl.when(jnp.logical_not(first))
     def _():
-        for t in range(8):
+        for t in range(32 // SPAN):
             pltpu.make_async_copy(group(t), group(t), ac_in.at[t]).wait()
 
     col_lab = labels(
@@ -330,18 +361,18 @@
 
     @pl.when(owner)
     def _():
-        for g in range(4):
+        for g in range(16 // SPAN):
             @pl.when(ylo == yhi)
             def _():
-                pltpu.make_async_copy(ac.at[pl.ds(0, 28)], ac.at[pl.ds(0, 28)], ac_out.at[g]).wait()
+                pltpu.make_async_copy(ac.at[pl.ds(0, 7 * SPAN)], ac.at[pl.ds(0, 7 * SPAN)], ac_out.at[g]).wait()
 
             @pl.when(ylo != yhi)
             def _():
-                pltpu.make_async_copy(ac, ac, ac_out.at[g]).wait()
+                pltpu.make_async_copy(ac.at[pl.ds(0, 8 * SPAN)], ac.at[pl.ds(0, 8 * SPAN)], ac_out.at[g]).wait()
 
     @pl.when(first)
     def _():
-        for t in range(8):
+        for t in range(32 // SPAN):
             pltpu.make_async_copy(group(t), group(t), pair_out.at[t]).wait()
 
 
@@ -362,8 +393,9 @@
             pltpu.VMEM((512, 128), jnp.int32),
             pltpu.SMEM((8,), jnp.int32),
             pltpu.SMEM((8,), jnp.int32),
-            dma((8,)), dma((16,)), dma, dma, dma((8,)), dma,
-            dma((MOST,)), dma, dma, dma, dma((4,)), dma((8,)),
+            dma((8,)), dma((16,)), dma, dma, dma((32 // SPAN,)), dma,
+            pltpu.SemaphoreType.REGULAR((2,)),
+            dma((MOST,)), dma, dma, dma, dma((16 // SPAN,)), dma((32 // SPAN,)),
         ],
         compiler_params=pltpu.CompilerParams(
             collective_id=0, has_side_effects=True, vmem_limit_bytes=32 * 2**20

time: 41.9 us -> 40.1 us (0.957)
  the two profiles are of different devices: /device:TPU:12 before, /device:TPU:109 now
where the time goes in v3:
time: 40.1 us; the launch traced here: 40 us
  Pallas kernels  39.2 us (98%)
  local copies, waits for them, and re-layouts  0.8 us (2%)
    pallas_call x1, Pallas kernels, per_device(): pl.pallas_call(kernel, out_shape=jax.ShapeDtypeStruct((512, 256), F32), i...  39.2 us

profile of v3, /device:TPU:109, one launch (start us, length us, event | category | flops | bytes accessed | tf_op | source)
XLA Modules:
  0.0 40.0 jit_solution(14644821108110934282)
XLA Ops:
  0.0 39.2 %shard_map.46 = f32[512,256]{1,0:T(8,128)S(1)} custom-call(f32[8,512]{1,0:T(8,128)} %bitcast.1, f32[16,256]{1,0:T(8,128)} %b_hbm.1, s32[8]{0:T(128)} %occ_hbm.1, s32[8]{0:T(128)} %vir_hbm.1), custom_call_target="tpu_custom_call" | custom-call | tf_op jit(solution)/shard_map/pallas_call | solution.py:383
  39.2 0.8 %copy.6 = f32[512,256]{1,0:T(8,128)} copy(f32[512,256]{1,0:T(8,128)S(1)} %shard_map.46) | data formatting | bytes 1048576

commit v4 on v3

--- a/solution.py
+++ b/solution.py
@@ -7,43 +7,44 @@
 
 NVIR = 400
 SPAN = 2
+SHARE_AFTER = 13
 MESH = pl.DeviceIdType.MESH
 F32 = jnp.float32
 BF16 = jnp.bfloat16
 
 TREE = (
-    (0x0000dc20, 0x000002cf, 0x000000f4, 0x000000d2, 0x0000031d, 0x0000e21b, 0x000000f3, 0x000000f6,
-     0x0000001a, 0x0000000e, 0x00000018, 0x000000d5, 0x00000001, 0x0000000c, 0x00000009, 0x00000007),
-    (0x11124bf1, 0x11111112, 0x1111204e, 0x11111105, 0x111d320c, 0x11111114, 0x11111119, 0x11111110,
-     0x1111112d, 0x11111113, 0x111113db, 0x1111116f, 0x111111d6, 0x1111111a, 0x11111118, 0x111111f7),
-    (0x22213042, 0x22222214, 0x22223510, 0x22222213, 0x22222221, 0x22222136, 0x2222222f, 0x22222235,
-     0x22222228, 0x2222222e, 0x222222f9, 0x222222ec, 0x2222222b, 0x22222227, 0x2222222d, 0x2222222a),
-    (0x33504623, 0x33333334, 0x33333382, 0x3333351f, 0x33321407, 0x33333348, 0x33333330, 0x33333339,
-     0x33333346, 0x33333331, 0x3333334d, 0x333333fa, 0x33333335, 0x3333333c, 0x3333333e, 0x3333333b),
-    (0x44532604, 0x44444425, 0x44444462, 0x44444443, 0x44447531, 0x4444235a, 0x4444653e, 0x44444449,
-     0x44444457, 0x4444444c, 0x44444458, 0x44444440, 0x4444444f, 0x44444446, 0x4444444d, 0x4444444b),
-    (0x55574615, 0x55555574, 0x55555553, 0x55555540, 0x55555559, 0x5555547f, 0x55555561, 0x5555555c,
-     0x5555555a, 0x55555552, 0x55555556, 0x5555555e, 0x5555555b, 0x55555557, 0x5555555d, 0x55555558),
-    (0x66662806, 0x66666895, 0x66666684, 0x66666329, 0x66666973, 0x6666574c, 0x66666572, 0x6666687a,
-     0x6666664b, 0x6666667d, 0x66666661, 0x66666668, 0x6666666e, 0x66666660, 0x66666667, 0x6666666f),
-    (0x7779e3a7, 0x777777a5, 0x7777b459, 0x77777774, 0x77777596, 0x7777775b, 0x7777b8a3, 0x77777768,
-     0x7777777c, 0x777777a2, 0x7777777e, 0x77778a91, 0x7777777f, 0x7777777a, 0x7777777d, 0x77777770),
-    (0x8893b028, 0x8888c7a6, 0x88888889, 0x8888886b, 0x888888b5, 0x888888a4, 0x8888885d, 0x88888867,
-     0x88888892, 0x88888883, 0x8888888c, 0x8888888a, 0x88888880, 0x8888888e, 0x8888888f, 0x88888881),
-    (0x998a7169, 0x9999a78b, 0x9999996a, 0x99999a78, 0x99999987, 0x99999995, 0x999999bd, 0x99999990,
-     0x999999c3, 0x9999999e, 0x99999996, 0x9999999c, 0x99999992, 0x99999991, 0x9999999f, 0x99999994),
-    (0xaaac940a, 0xaaaaac09, 0xaaaaa86d, 0xaaaaaab7, 0xaaaaaacb, 0xaaaaa97e, 0xaaaaaaa8, 0xaaaaaaa6,
-     0xaaaaa98c, 0xaaaaaaf5, 0xaaaaa870, 0xaaaaa98f, 0xaaaaa9b4, 0xaaaaaaa3, 0xaaaaaaa2, 0xaaaaaaa1),
-    (0xbbbbb09b, 0xbbbbbbac, 0xbbbbbed8, 0xbbbbbbce, 0xbbbbbb60, 0xbbbbbdc7, 0xbbbbbbba, 0xbbbbbbb1,
-     0xbbbbbbb9, 0xbbbbbbc5, 0xbbbbbbbf, 0xbbbbbbb2, 0xbbbbbbbd, 0xbbbbbbb6, 0xbbbbbbb3, 0xbbbbbbb4),
-    (0xccccb16c, 0xccccc9ed, 0xccccc9b0, 0xcccccbda, 0xccccccbf, 0xccccccd9, 0xcccccc8e, 0xccccccb6,
-     0xcccccccb, 0xccccccc7, 0xccccccc2, 0xccccccc8, 0xccccccc1, 0xccccccc4, 0xccccccc5, 0xccccccc3),
-    (0xddddca0d, 0xdddddabe, 0xdddddea0, 0xddddddaf, 0xddddddea, 0xdddfecb2, 0xddddddc8, 0xdddddec1,
-     0xddddddc4, 0xdddddde9, 0xddddddfc, 0xdddddde5, 0xddddddd7, 0xdddddddb, 0xddddddd6, 0xddddddd3),
-    (0xeeeed1fe, 0xeeeeeedf, 0xeeeeeefd, 0xeeeeeef0, 0xeeeeeefb, 0xeeeeeee7, 0xeeeeeee4, 0xeeeeeef8,
-     0xeeeeeeea, 0xeeeeeee2, 0xeeeeeed3, 0xeeeeeee1, 0xeeeeeee6, 0xeeeeeee9, 0xeeeeeeec, 0xeeeeeee5),
-    (0xffff3e0f, 0xfffffffe, 0xfffffd01, 0xfffffed4, 0xffffffe3, 0xffffffe6, 0xfffffffd, 0xfffffff0,
-     0xfffffffb, 0xfffffff2, 0xfffffff9, 0xfffffff8, 0xfffffff7, 0xfffffff5, 0xfffffffa, 0xfffffffc),
+    (0x002fd1e0, 0x000000f4, 0x000000c1, 0x0000001f, 0x000000e3, 0x0000013e, 0x000000f5, 0x00000df2,
+     0x00000e1b, 0x00000d19, 0x0000003c, 0x00000fed, 0x00000007, 0x0000000a, 0x000000d8, 0x00000ef6),
+    (0x11142f01, 0x11111032, 0x11111113, 0x11111130, 0x11111114, 0x11111115, 0x1111120d, 0x11111107,
+     0x1111111f, 0x1111203a, 0x1111112e, 0x1111123b, 0x111111fc, 0x11111119, 0x111111f8, 0x11111116),
+    (0x22226412, 0x22222224, 0x22222361, 0x22222223, 0x22222240, 0x22222347, 0x2222222f, 0x22222225,
+     0x22222208, 0x2222243d, 0x22222229, 0x2222222a, 0x22222246, 0x2222222e, 0x2222222c, 0x2222222b),
+    (0x33264013, 0x33333614, 0x33333425, 0x3333364f, 0x33333351, 0x33333332, 0x33351206, 0x33333350,
+     0x33333338, 0x3333345e, 0x33333339, 0x33333337, 0x3333333a, 0x3333333d, 0x3333333c, 0x3333333b),
+    (0x44430254, 0x44444453, 0x44444452, 0x44444441, 0x44443529, 0x44444445, 0x4444445f, 0x44444440,
+     0x4444444a, 0x44444447, 0x4444444b, 0x4444444c, 0x4444444e, 0x4444444d, 0x44444448, 0x44444446),
+    (0x55613705, 0x55555574, 0x55555553, 0x55555572, 0x5555547b, 0x5555524c, 0x55555769, 0x55555571,
+     0x55555558, 0x5555555f, 0x55555556, 0x55555760, 0x5555555d, 0x5555555e, 0x55555557, 0x5555555a),
+    (0x66666736, 0x66666665, 0x66667d93, 0x66666692, 0x66666664, 0x66666661, 0x6666666d, 0x66666648,
+     0x6666667f, 0x66666657, 0x6666665a, 0x666666e9, 0x6666666c, 0x6666666b, 0x66666660, 0x6666666e),
+    (0x77728917, 0x77777985, 0x77777784, 0x77777568, 0x77777786, 0x77777783, 0x77777772, 0x7777776c,
+     0x7777768b, 0x7777779e, 0x7777777d, 0x7777778f, 0x77777779, 0x77777771, 0x7777777a, 0x77777770),
+    (0x8897c328, 0x8888884a, 0x88888887, 0x888888b5, 0x88888894, 0x88888889, 0x8889bcd6, 0x88888883,
+     0x8888888c, 0x8888888d, 0x88888882, 0x8888888b, 0x8888888f, 0x88888880, 0x88888881, 0x8888888e),
+    (0x999c0a49, 0x99996ca7, 0x99999b6a, 0x999999ab, 0x99999998, 0x999999c5, 0x999999a3, 0x9999997d,
+     0x99999994, 0x99999982, 0x9999999c, 0x999999cf, 0x999999a6, 0x9999998e, 0x99999990, 0x99999991),
+    (0xaaac198a, 0xaaaaaa89, 0xaaaaaaa7, 0xaaaaa98c, 0xaaaaaa8d, 0xaaaaaacb, 0xaaaaaa6e, 0xaaaaabc3,
+     0xaaaaa890, 0xaaaaaaa8, 0xaaaaa891, 0xaaaaaac4, 0xaaaaaaa5, 0xaaaaaaaf, 0xaaaaaaa6, 0xaaaaaaa2),
+    (0xbbbb509b, 0xbbbbba7c, 0xbbbb5a9d, 0xbbbbbb7e, 0xbbbbbd9f, 0xbbbbbb7a, 0xbbbbbac0, 0xbbbbbae8,
+     0xbbbbbbd5, 0xbbbbbbb7, 0xbbbbbbb1, 0xbbbbbbb4, 0xbbbbbbb3, 0xbbbbbba2, 0xbbbbbbb6, 0xbbbbbbb9),
+    (0xcccc5bdc, 0xccccceda, 0xcccccccd, 0xccccccf9, 0xcccccb18, 0xcccccafe, 0xccccdeb7, 0xcccccda1,
+     0xcccccae5, 0xccccccc0, 0xcccccccb, 0xccccccc2, 0xccccccc6, 0xccccccc3, 0xcccccccf, 0xccccccc4),
+    (0xdddc16bd, 0xddddd10c, 0xddddddce, 0xddddddb0, 0xddddddfa, 0xdddddba4, 0xddddebc2, 0xddddddaf,
+     0xddddddb9, 0xddddddf7, 0xddddddd1, 0xddddddf3, 0xdddddddb, 0xddddddd8, 0xddddddd5, 0xddddddd6),
+    (0xeeeedb0e, 0xeeeeeebf, 0xeeeeeee0, 0xeeeeeee3, 0xeeeeeeb1, 0xeeeeeeea, 0xeeeeeee4, 0xeeeeedfb,
+     0xeeeeeee7, 0xeeeeeeed, 0xeeeeeee2, 0xeeeeeee8, 0xeeeeeee5, 0xeeeeeee6, 0xeeeeeeec, 0xeeeeeee9),
+    (0xfff20e3f, 0xfffffff0, 0xffffffe1, 0xfffffed4, 0xfffffff5, 0xfffffff2, 0xfffffff9, 0xfffffffa,
+     0xfffffffe, 0xfffffffd, 0xffffffec, 0xfffffffb, 0xfffffff6, 0xfffffff8, 0xfffffff7, 0xfffffff3),
 )
 
 def signed(word):
@@ -122,8 +123,8 @@
 def kernel(
     a_hbm, b_hbm, occ_hbm, vir_hbm, o_ref,
     w, br, bc, ac, row_lab, occ, vir,
-    local, w_in, br_in, bc_in, ac_in, cross_in, ready,
-    tree_out, cross_out, br_out, bc_out, ac_out, pair_out,
+    local, w_in, br_in, bc_in, ac_in, cross_in, ap_in, share_in, ready,
+    tree_out, cross_out, br_out, bc_out, ac_out, pair_out, ap_out, share_out,
 ):
     row = lax.axis_index("row")
     col = lax.axis_index("col")
@@ -189,7 +190,21 @@
 
     lax.fori_loop(0, 16, greet_z, 0)
 
-    pl.semaphore_wait(barrier, jnp.where(late, 7, 31) + by_z(z, TARGETS))
+    share = ylo * 8 + (x - z // 4 + 6) % 4 * 2 + core
+    early = jnp.logical_not(late)
+    shares = jnp.logical_and(early, share % 8 >= 4)
+    direct = jnp.logical_and(late, x < 2)
+
+    @pl.when(shares)
+    def _():
+        for e in (0, 1):
+            pl.semaphore_signal(
+                barrier, inc=1, device_id={"row": col // 2, "col": 2 * share + e}, device_id_type=MESH
+            )
+
+    pl.semaphore_wait(
+        barrier, jnp.where(late, 7, 31) + by_z(z, TARGETS) + 2 * direct.astype(jnp.int32)
+    )
 
     @pl.when(late)
     def _():
@@ -255,6 +270,15 @@
             return carry
 
         lax.fori_loop(0, 8, one, 0)
+
+    def direct_to(h):
+        r = yhi * 8 + (x + z // 4 + 2) % 4 * 2 + z // 2 % 2
+        return pltpu.make_async_remote_copy(
+            src_ref=w.at[col, h], dst_ref=ac.at[col], send_sem=ap_out.at[h], recv_sem=ap_in,
+            device_id={"row": r, "col": 2 * row + h}, device_id_type=MESH,
+        )
+
+    share_piece = ac.at[pl.ds(2 * share, 2)]
 
     last = by_z(z, LAST)
     sent = jnp.int32(0)
@@ -275,6 +299,11 @@
 
         sent = lax.fori_loop(1, 8, forward, sent)
         if k == 0:
+            @pl.when(direct)
+            def _():
+                direct_to(0).start()
+                direct_to(1).start()
+
             @pl.when(late)
             def _():
                 pl.semaphore_wait(ready.at[0], 7)
@@ -284,7 +313,9 @@
         to_rows(s, 0)
         to_rows(s, 1)
 
-        @pl.when(jnp.logical_and(owner, ((last >> k) & 1) == 1))
+        @pl.when(
+            jnp.logical_and(jnp.logical_and(owner, ((last >> k) & 1) == 1), jnp.logical_or(late, s < 8))
+        )
         def _():
             to_plane(s // SPAN)
 
@@ -304,14 +335,30 @@
             row_pos = row * 512 + lax.broadcasted_iota(jnp.int32, (512, 128), 0)
             row_lab[...] = labels(row_pos, row * 512, occ, vir)
 
+        if k == SHARE_AFTER:
+            @pl.when(shares)
+            def _():
+                pltpu.make_async_copy(share_piece, share_piece, ap_in).wait()
+
+                def give_share(r, carry):
+                    @pl.when(r != row)
+                    def _():
+                        pltpu.make_async_remote_copy(
+                            src_ref=share_piece, dst_ref=share_piece, send_sem=share_out,
+                            recv_sem=share_in, device_id={"row": r, "col": col}, device_id_type=MESH,
+                        ).start()
+                    return carry
+
+                lax.fori_loop(0, 16, give_share, 0)
+
     first = core == (z // 2) % 2
 
     def group(t):
         return ac.at[pl.ds(SPAN * t, SPAN)]
 
-    @pl.when(first)
-    def _():
-        for g in GROUPS:
+    for g in GROUPS:
+        @pl.when(jnp.logical_and(first, late) if g * SPAN >= 8 else first)
+        def _():
             for y in (0, 1):
                 t = 16 // SPAN * y + g
                 pltpu.make_async_copy(group(t), group(t), ac_in.at[t]).wait()
@@ -323,21 +370,34 @@
 
     pltpu.make_async_copy(bc.at[pl.ds(0, 15)], bc.at[pl.ds(0, 15)], bc_in).wait()
     pltpu.make_async_copy(ac, ac, cross_in).wait()
+    b_here = bc[...].reshape(256, 256)
+    for m in (0, 1):
+        o_ref[256 * m : 256 * (m + 1)] = product(w[:, m].reshape(256, 256), b_here)
+
     pltpu.make_async_copy(br, br, br_in).wait()
 
-    @pl.when(jnp.logical_not(first))
-    def _():
-        for t in range(32 // SPAN):
+    for t in range(32 // SPAN):
+        here = jnp.logical_not(first)
+
+        @pl.when(jnp.logical_and(here, late) if t * SPAN % 16 >= 8 else here)
+        def _():
             pltpu.make_async_copy(group(t), group(t), ac_in.at[t]).wait()
+
+    @pl.when(shares)
+    def _():
+        pltpu.make_async_copy(ac.at[pl.ds(0, 14)], ac.at[pl.ds(0, 14)], share_in).wait()
+
+    @pl.when(jnp.logical_and(early, jnp.logical_not(shares)))
+    def _():
+        pltpu.make_async_copy(ac.at[pl.ds(0, 16)], ac.at[pl.ds(0, 16)], share_in).wait()
 
     col_lab = labels(
         col * 256 + lax.broadcasted_iota(jnp.int32, (8, 256), 1), col * 256, occ, vir
     )[:1]
-    b_here = bc[...].reshape(256, 256)
     a_here = ac[...].reshape(256, 256)
     for m in (0, 1):
         rows = slice(256 * m, 256 * (m + 1))
-        total = product(w[:, m].reshape(256, 256), b_here) + product(br[:, m].reshape(256, 256), a_here)
+        total = o_ref[rows] + product(br[:, m].reshape(256, 256), a_here)
         lab = row_lab[rows]
         for h in (0, 1):
             lanes = slice(128 * h, 128 * (h + 1))
@@ -359,21 +419,30 @@
     def _():
         pltpu.make_async_copy(br, br, br_out).wait()
 
-    @pl.when(owner)
-    def _():
-        for g in range(16 // SPAN):
-            @pl.when(ylo == yhi)
-            def _():
-                pltpu.make_async_copy(ac.at[pl.ds(0, 7 * SPAN)], ac.at[pl.ds(0, 7 * SPAN)], ac_out.at[g]).wait()
-
-            @pl.when(ylo != yhi)
-            def _():
-                pltpu.make_async_copy(ac.at[pl.ds(0, 8 * SPAN)], ac.at[pl.ds(0, 8 * SPAN)], ac_out.at[g]).wait()
-
-    @pl.when(first)
-    def _():
-        for t in range(32 // SPAN):
+    for g in range(16 // SPAN):
+        gave = jnp.logical_and(owner, late) if g * SPAN >= 8 else owner
+
+        @pl.when(jnp.logical_and(gave, ylo == yhi))
+        def _():
+            pltpu.make_async_copy(ac.at[pl.ds(0, 7 * SPAN)], ac.at[pl.ds(0, 7 * SPAN)], ac_out.at[g]).wait()
+
+        @pl.when(jnp.logical_and(gave, ylo != yhi))
+        def _():
+            pltpu.make_async_copy(ac.at[pl.ds(0, 8 * SPAN)], ac.at[pl.ds(0, 8 * SPAN)], ac_out.at[g]).wait()
+
+    for t in range(32 // SPAN):
+        @pl.when(jnp.logical_and(first, late) if t * SPAN % 16 >= 8 else first)
+        def _():
             pltpu.make_async_copy(group(t), group(t), pair_out.at[t]).wait()
+
+    @pl.when(direct)
+    def _():
+        direct_to(0).wait_send()
+        direct_to(1).wait_send()
+
+    @pl.when(shares)
+    def _():
+        pltpu.make_async_copy(ac.at[pl.ds(0, 30)], ac.at[pl.ds(0, 30)], share_out).wait()
 
 
 def per_device(amplitudes, integrals, occ_counts, vir_counts):
@@ -394,8 +463,8 @@
             pltpu.SMEM((8,), jnp.int32),
             pltpu.SMEM((8,), jnp.int32),
             dma((8,)), dma((16,)), dma, dma, dma((32 // SPAN,)), dma,
-            pltpu.SemaphoreType.REGULAR((2,)),
-            dma((MOST,)), dma, dma, dma, dma((16 // SPAN,)), dma((32 // SPAN,)),
+            dma, dma, pltpu.SemaphoreType.REGULAR((2,)),
+            dma((MOST,)), dma, dma, dma, dma((16 // SPAN,)), dma((32 // SPAN,)), dma((2,)), dma,
         ],
         compiler_params=pltpu.CompilerParams(
             collective_id=0, has_side_effects=True, vmem_limit_bytes=32 * 2**20

time: 40.1 us -> 38.3 us (0.955)
  the two profiles are of different devices: /device:TPU:109 before, /device:TPU:43 now
where the time goes in v4:
time: 38.3 us; the launch traced here: 38.2 us
  Pallas kernels  37.4 us (98%)
  local copies, waits for them, and re-layouts  0.8 us (2%)
    pallas_call x1, Pallas kernels, per_device(): pl.pallas_call(kernel, out_shape=jax.ShapeDtypeStruct((512, 256), F32), i...  37.4 us
    unnamed x1, local copies, waits for them, and re-layouts  0.8 us

profile of v4, /device:TPU:43, one launch (start us, length us, event | category | flops | bytes accessed | tf_op | source)
XLA Modules:
  0.0 38.2 jit_solution(9413605032671921760)
XLA Ops:
  0.0 37.4 %shard_map.46 = f32[512,256]{1,0:T(8,128)S(1)} custom-call(f32[8,512]{1,0:T(8,128)} %bitcast.1, f32[16,256]{1,0:T(8,128)} %b_hbm.1, s32[8]{0:T(128)} %occ_hbm.1, s32[8]{0:T(128)} %vir_hbm.1), custom_call_target="tpu_custom_call" | custom-call | tf_op jit(solution)/shard_map/pallas_call | solution.py:452
  37.4 0.8 %copy.6 = f32[512,256]{1,0:T(8,128)} copy(f32[512,256]{1,0:T(8,128)S(1)} %shard_map.46) | data formatting | bytes 1048576

commit v5 on v4

--- a/solution.py
+++ b/solution.py
@@ -7,7 +7,7 @@
 
 NVIR = 400
 SPAN = 2
-SHARE_AFTER = 13
+SHARE_AFTER = 10
 MESH = pl.DeviceIdType.MESH
 F32 = jnp.float32
 BF16 = jnp.bfloat16
@@ -79,7 +79,6 @@
 
 
 SENDS = [sum((word >> (4 * k)) & 15 != z for word in TREE[z] for k in range(1, 8)) for z in range(16)]
-MOST = max(SENDS)
 TARGETS = [len(targets(z)) for z in range(16)]
 LAST = [
     sum(1 << k for k in range(16) if all(TREE[z][i] & 15 != q for i in range(k + 1, 16) for q in quarter(TREE[z][k])))
@@ -135,21 +134,18 @@
     x = row // 2 % 4
 
     own = [
-        pltpu.make_async_copy(a_hbm.at[:, pl.ds(256 * h, 256)], w.at[col, h], local.at[h])
+        pltpu.make_async_copy(a_hbm.at[:, pl.ds(256 * h, 256)], w.at[col, h], local.at[0])
         for h in (0, 1)
     ] + [
-        pltpu.make_async_copy(b_hbm.at[pl.ds(8 * h, 8)], w.at[col, 2 + h], local.at[2 + h])
+        pltpu.make_async_copy(b_hbm.at[pl.ds(8 * h, 8)], w.at[col, 2 + h], local.at[0])
         for h in (0, 1)
     ]
     small = [
-        pltpu.make_async_copy(occ_hbm, occ, local.at[4]),
-        pltpu.make_async_copy(vir_hbm, vir, local.at[5]),
-        pltpu.make_async_copy(b_hbm.at[pl.ds(0, 8)], bc.at[row, 0], local.at[6]),
-        pltpu.make_async_copy(b_hbm.at[pl.ds(8, 8)], bc.at[row, 1], local.at[7]),
+        pltpu.make_async_copy(occ_hbm, occ, local.at[2]),
+        pltpu.make_async_copy(vir_hbm, vir, local.at[3]),
+        pltpu.make_async_copy(b_hbm.at[pl.ds(0, 8)], bc.at[row, 0], local.at[1]),
+        pltpu.make_async_copy(b_hbm.at[pl.ds(8, 8)], bc.at[row, 1], local.at[1]),
     ]
-    for copy in own + small:
-        copy.start()
-
     barrier = pltpu.get_barrier_semaphore()
     sources = by_z(z, SOURCES)
 
@@ -189,6 +185,8 @@
         lax.fori_loop(0, 32, greet_plane, 0)
 
     lax.fori_loop(0, 16, greet_z, 0)
+    for copy in own + small:
+        copy.start()
 
     share = ylo * 8 + (x - z // 4 + 6) % 4 * 2 + core
     early = jnp.logical_not(late)
@@ -202,6 +200,17 @@
                 barrier, inc=1, device_id={"row": col // 2, "col": 2 * share + e}, device_id_type=MESH
             )
 
+    def label_rows():
+        small[0].wait()
+        small[1].wait()
+        pltpu.make_async_copy(bc.at[0], bc.at[0], local.at[1]).wait()
+        row_pos = row * 512 + lax.broadcasted_iota(jnp.int32, (512, 128), 0)
+        row_lab[...] = labels(row_pos, row * 512, occ, vir)
+
+    @pl.when(early)
+    def _():
+        label_rows()
+
     pl.semaphore_wait(
         barrier, jnp.where(late, 7, 31) + by_z(z, TARGETS) + 2 * direct.astype(jnp.int32)
     )
@@ -211,13 +220,12 @@
         for peer in peers:
             pl.semaphore_signal(ready.at[0], inc=1, device_id=peer, device_id_type=MESH)
 
-    for copy in own:
-        copy.wait()
-
-    def send_tree(s, d, j):
+    pltpu.make_async_copy(w.at[0], w.at[0], local.at[0]).wait()
+
+    def send_tree(s, d):
         c = yhi * 16 + s
         pltpu.make_async_remote_copy(
-            src_ref=w.at[c], dst_ref=w.at[c], send_sem=tree_out.at[j], recv_sem=w_in.at[s],
+            src_ref=w.at[c], dst_ref=w.at[c], send_sem=tree_out, recv_sem=w_in.at[s],
             device_id={"row": row, "col": yhi * 16 + d}, device_id_type=MESH,
         ).start()
 
@@ -263,7 +271,7 @@
             @pl.when(jnp.logical_not(me))
             def _():
                 pltpu.make_async_remote_copy(
-                    src_ref=source, dst_ref=ac.at[pl.ds(c, SPAN)], send_sem=ac_out.at[g],
+                    src_ref=source, dst_ref=ac.at[pl.ds(c, SPAN)], send_sem=ac_out,
                     recv_sem=ac_in.at[t],
                     device_id={"row": r, "col": ylo * 16 + z}, device_id_type=MESH,
                 ).start()
@@ -274,50 +282,50 @@
     def direct_to(h):
         r = yhi * 8 + (x + z // 4 + 2) % 4 * 2 + z // 2 % 2
         return pltpu.make_async_remote_copy(
-            src_ref=w.at[col, h], dst_ref=ac.at[col], send_sem=ap_out.at[h], recv_sem=ap_in,
+            src_ref=w.at[col, h], dst_ref=ac.at[col], send_sem=ap_out, recv_sem=ap_in,
             device_id={"row": r, "col": 2 * row + h}, device_id_type=MESH,
         )
 
     share_piece = ac.at[pl.ds(2 * share, 2)]
 
+    @pl.when(direct)
+    def _():
+        direct_to(0).start()
+        direct_to(1).start()
+
     last = by_z(z, LAST)
-    sent = jnp.int32(0)
     for k in range(16):
         word = by_z(z, [TREE[v][k] for v in range(16)])
         s = nibble(word, 0)
         if k:
             pltpu.make_async_copy(w.at[s], w.at[s], w_in.at[s]).wait()
 
-        def forward(i, j):
+        def forward(i, carry):
             d = (word >> (4 * i)) & 15
             there = d != z
 
             @pl.when(there)
             def _():
-                send_tree(s, d, j)
-            return j + there.astype(jnp.int32)
-
-        sent = lax.fori_loop(1, 8, forward, sent)
+                send_tree(s, d)
+            return carry
+
+        lax.fori_loop(1, 8, forward, 0)
         if k == 0:
-            @pl.when(direct)
-            def _():
-                direct_to(0).start()
-                direct_to(1).start()
-
             @pl.when(late)
             def _():
                 pl.semaphore_wait(ready.at[0], 7)
                 pl.semaphore_signal(ready.at[1], inc=1, device_id=other, device_id_type=MESH)
                 pl.semaphore_wait(ready.at[1], 1)
+        @pl.when(
+            jnp.logical_and(jnp.logical_and(owner, ((last >> k) & 1) == 1), jnp.logical_or(late, s < 8))
+        )
+        def _():
+            to_plane(s // SPAN)
+
         cross(s).start()
         to_rows(s, 0)
         to_rows(s, 1)
 
-        @pl.when(
-            jnp.logical_and(jnp.logical_and(owner, ((last >> k) & 1) == 1), jnp.logical_or(late, s < 8))
-        )
-        def _():
-            to_plane(s // SPAN)
 
         if k == 0:
             def give(r, carry):
@@ -330,10 +338,10 @@
                 return carry
 
             lax.fori_loop(0, 16, give, 0)
-            for copy in small:
-                copy.wait()
-            row_pos = row * 512 + lax.broadcasted_iota(jnp.int32, (512, 128), 0)
-            row_lab[...] = labels(row_pos, row * 512, occ, vir)
+
+            @pl.when(late)
+            def _():
+                label_rows()
 
         if k == SHARE_AFTER:
             @pl.when(shares)
@@ -363,7 +371,7 @@
                 t = 16 // SPAN * y + g
                 pltpu.make_async_copy(group(t), group(t), ac_in.at[t]).wait()
                 pltpu.make_async_remote_copy(
-                    src_ref=group(t), dst_ref=group(t), send_sem=pair_out.at[t],
+                    src_ref=group(t), dst_ref=group(t), send_sem=pair_out,
                     recv_sem=ac_in.at[t], device_id={"row": 2 * (row // 2) + 1 - core, "col": col},
                     device_id_type=MESH,
                 ).start()
@@ -403,11 +411,12 @@
             lanes = slice(128 * h, 128 * (h + 1))
             o_ref[rows, lanes] = jnp.where(lab == col_lab[:, lanes], total[:, lanes], 0.0)
 
-    def sent_tree(j, carry):
-        pltpu.make_async_copy(w.at[0], w.at[0], tree_out.at[j]).wait()
-        return carry
-
-    lax.fori_loop(0, by_z(z, SENDS), sent_tree, 0)
+    count = by_z(z, SENDS)
+    for n in sorted(set(SENDS)):
+        @pl.when(count == n)
+        def _():
+            pltpu.make_async_copy(w.at[pl.ds(0, n)], w.at[pl.ds(0, n)], tree_out).wait()
+
     pltpu.make_async_copy(ac, ac, cross_out).wait()
     pltpu.make_async_copy(bc.at[pl.ds(0, 15)], bc.at[pl.ds(0, 15)], bc_out).wait()
 
@@ -419,26 +428,20 @@
     def _():
         pltpu.make_async_copy(br, br, br_out).wait()
 
-    for g in range(16 // SPAN):
-        gave = jnp.logical_and(owner, late) if g * SPAN >= 8 else owner
-
-        @pl.when(jnp.logical_and(gave, ylo == yhi))
-        def _():
-            pltpu.make_async_copy(ac.at[pl.ds(0, 7 * SPAN)], ac.at[pl.ds(0, 7 * SPAN)], ac_out.at[g]).wait()
-
-        @pl.when(jnp.logical_and(gave, ylo != yhi))
-        def _():
-            pltpu.make_async_copy(ac.at[pl.ds(0, 8 * SPAN)], ac.at[pl.ds(0, 8 * SPAN)], ac_out.at[g]).wait()
-
-    for t in range(32 // SPAN):
-        @pl.when(jnp.logical_and(first, late) if t * SPAN % 16 >= 8 else first)
-        def _():
-            pltpu.make_async_copy(group(t), group(t), pair_out.at[t]).wait()
+    for when, chips in ((ylo == yhi, 7), (ylo != yhi, 8)):
+        for plane, pieces in ((early, 2 * chips), (late, 4 * chips)):
+            @pl.when(jnp.logical_and(owner, jnp.logical_and(when, plane)))
+            def _():
+                pltpu.make_async_copy(w.at[pl.ds(0, pieces)], w.at[pl.ds(0, pieces)], ac_out).wait()
+
+    for plane, pieces in ((early, 16), (late, 32)):
+        @pl.when(jnp.logical_and(first, plane))
+        def _():
+            pltpu.make_async_copy(ac.at[pl.ds(0, pieces)], ac.at[pl.ds(0, pieces)], pair_out).wait()
 
     @pl.when(direct)
     def _():
-        direct_to(0).wait_send()
-        direct_to(1).wait_send()
+        pltpu.make_async_copy(ac.at[pl.ds(0, 2)], ac.at[pl.ds(0, 2)], ap_out).wait()
 
     @pl.when(shares)
     def _():
@@ -462,9 +465,9 @@
             pltpu.VMEM((512, 128), jnp.int32),
             pltpu.SMEM((8,), jnp.int32),
             pltpu.SMEM((8,), jnp.int32),
-            dma((8,)), dma((16,)), dma, dma, dma((32 // SPAN,)), dma,
+            dma((4,)), dma((16,)), dma, dma, dma((32 // SPAN,)), dma,
             dma, dma, pltpu.SemaphoreType.REGULAR((2,)),
-            dma((MOST,)), dma, dma, dma, dma((16 // SPAN,)), dma((32 // SPAN,)), dma((2,)), dma,
+            dma, dma, dma, dma, dma, dma, dma, dma,
         ],
         compiler_params=pltpu.CompilerParams(
             collective_id=0, has_side_effects=True, vmem_limit_bytes=32 * 2**20

time: 38.3 us -> 37.7 us (0.984)
  Pallas kernels: 37.4 us -> 36.7 us
    pallas_call x1, Pallas kernels: 37.4 us -> 36.7 us  [per_device(): pl.pallas_call(kernel, out_shape=jax.ShapeDtypeStruct((512, 256), F32), i...]
where the time goes in v5:
time: 37.7 us; the launch traced here: 37.5 us
  Pallas kernels  36.7 us (97%)
  local copies, waits for them, and re-layouts  0.8 us (2%)
    pallas_call x1, Pallas kernels, per_device(): pl.pallas_call(kernel, out_shape=jax.ShapeDtypeStruct((512, 256), F32), i...  36.7 us
    unnamed x1, local copies, waits for them, and re-layouts  0.8 us

profile of v5, /device:TPU:43, one launch (start us, length us, event | category | flops | bytes accessed | tf_op | source)
XLA Modules:
  0.0 37.5 jit_solution(11869868674011426014)
XLA Ops:
  0.0 36.7 %shard_map.46 = f32[512,256]{1,0:T(8,128)S(1)} custom-call(f32[8,512]{1,0:T(8,128)} %bitcast.1, f32[16,256]{1,0:T(8,128)} %b_hbm.1, s32[8]{0:T(128)} %occ_hbm.1, s32[8]{0:T(128)} %vir_hbm.1), custom_call_target="tpu_custom_call" | custom-call | tf_op jit(solution)/shard_map/pallas_call | solution.py:455
  36.7 0.8 %copy.6 = f32[512,256]{1,0:T(8,128)} copy(f32[512,256]{1,0:T(8,128)S(1)} %shard_map.46) | data formatting | bytes 1048576

commit v6 on v5

--- a/solution.py
+++ b/solution.py
@@ -376,6 +376,10 @@
                     device_id_type=MESH,
                 ).start()
 
+    col_lab = labels(
+        col * 256 + lax.broadcasted_iota(jnp.int32, (8, 256), 1), col * 256, occ, vir
+    )[:1]
+
     pltpu.make_async_copy(bc.at[pl.ds(0, 15)], bc.at[pl.ds(0, 15)], bc_in).wait()
     pltpu.make_async_copy(ac, ac, cross_in).wait()
     b_here = bc[...].reshape(256, 256)
@@ -399,9 +403,6 @@
     def _():
         pltpu.make_async_copy(ac.at[pl.ds(0, 16)], ac.at[pl.ds(0, 16)], share_in).wait()
 
-    col_lab = labels(
-        col * 256 + lax.broadcasted_iota(jnp.int32, (8, 256), 1), col * 256, occ, vir
-    )[:1]
     a_here = ac[...].reshape(256, 256)
     for m in (0, 1):
         rows = slice(256 * m, 256 * (m + 1))

time: 37.7 us -> 37.7 us (level)
  no operation moved by 1% of the time
where the time goes in v6:
time: 37.7 us; the launch traced here: 37.5 us
  Pallas kernels  36.7 us (97%)
  local copies, waits for them, and re-layouts  0.8 us (2%)
    pallas_call x1, Pallas kernels, per_device(): pl.pallas_call(kernel, out_shape=jax.ShapeDtypeStruct((512, 256), F32), i...  36.7 us
    unnamed x1, local copies, waits for them, and re-layouts  0.8 us

profile of v6, /device:TPU:43, one launch (start us, length us, event | category | flops | bytes accessed | tf_op | source)
XLA Modules:
  0.0 37.5 jit_solution(15604186673042865178)
XLA Ops:
  0.0 36.7 %shard_map.46 = f32[512,256]{1,0:T(8,128)S(1)} custom-call(f32[8,512]{1,0:T(8,128)} %bitcast.1, f32[16,256]{1,0:T(8,128)} %b_hbm.1, s32[8]{0:T(128)} %occ_hbm.1, s32[8]{0:T(128)} %vir_hbm.1), custom_call_target="tpu_custom_call" | custom-call | tf_op jit(solution)/shard_map/pallas_call | solution.py:456
  36.7 0.8 %copy.6 = f32[512,256]{1,0:T(8,128)} copy(f32[512,256]{1,0:T(8,128)S(1)} %shard_map.46) | data formatting | bytes 1048576

commit v7 on v5

--- a/solution.py
+++ b/solution.py
@@ -339,9 +339,6 @@
 
             lax.fori_loop(0, 16, give, 0)
 
-            @pl.when(late)
-            def _():
-                label_rows()
 
         if k == SHARE_AFTER:
             @pl.when(shares)
@@ -375,6 +372,10 @@
                     recv_sem=ac_in.at[t], device_id={"row": 2 * (row // 2) + 1 - core, "col": col},
                     device_id_type=MESH,
                 ).start()
+
+    @pl.when(late)
+    def _():
+        label_rows()
 
     pltpu.make_async_copy(bc.at[pl.ds(0, 15)], bc.at[pl.ds(0, 15)], bc_in).wait()
     pltpu.make_async_copy(ac, ac, cross_in).wait()

time: 37.7 us -> 37.7 us (level)
  no operation moved by 1% of the time
where the time goes in v7:
time: 37.7 us; the launch traced here: 37.5 us
  Pallas kernels  36.7 us (97%)
  local copies, waits for them, and re-layouts  0.8 us (2%)
    pallas_call x1, Pallas kernels, per_device(): pl.pallas_call(kernel, out_shape=jax.ShapeDtypeStruct((512, 256), F32), i...  36.7 us
    unnamed x1, local copies, waits for them, and re-layouts  0.8 us

profile of v7, /device:TPU:43, one launch (start us, length us, event | category | flops | bytes accessed | tf_op | source)
XLA Modules:
  0.0 37.5 jit_solution(16783399027307429161)
XLA Ops:
  0.0 36.7 %shard_map.46 = f32[512,256]{1,0:T(8,128)S(1)} custom-call(f32[8,512]{1,0:T(8,128)} %bitcast.1, f32[16,256]{1,0:T(8,128)} %b_hbm.1, s32[8]{0:T(128)} %occ_hbm.1, s32[8]{0:T(128)} %vir_hbm.1), custom_call_target="tpu_custom_call" | custom-call | tf_op jit(solution)/shard_map/pallas_call | solution.py:456
  36.7 0.8 %copy.6 = f32[512,256]{1,0:T(8,128)} copy(f32[512,256]{1,0:T(8,128)S(1)} %shard_map.46) | data formatting | bytes 1048576
